TPU v7x, 128 devices: a whole 4x4x4 slice. The times are simulated.
128 devices in a mesh: lat: 8 (over x_hi, y), ang: 16 (over x_lo, z, core).
Axes of the slice: x: 4 (x_hi: 2, x_lo: 2; x = x_hi * 2 + x_lo), y: 4, z: 4, core: 2. Of those that a mesh axis runs over, the one named last changes fastest.
Arguments:
- incident: float32 [2, 256, 262144], P(None, 'ang', 'lat'), may hold values from -6 to 6
- detuning: float32 [256], P('ang'), may hold values from -1.5 to 1.5
- phase_table: int32 [3, 262144], P(None, 'lat'), may hold values from -32768 to 32767
- response: float32 [256, 256], replicated, may hold values from 0 to 2, as said below
- counts: int32 [256, 262144], P(None, ('lat', 'ang')), may hold values from 0 to 3
Outputs:
- exit_field: float32 [2, 256, 262144], P(None, 'ang', 'lat')
- estimate: float32 [256, 262144], P('ang', 'lat')
Inputs may be any that keep to these rules, and one draw needn't show every extreme that they name: `response`: every entry is positive.
All inputs are finite; a program needn't handle non-finite values.
Results may differ from a plain program's by a relative error of at most 0.00013.
Values sent between devices are 32-bit elements; how exact they have to be, the bound alone decides.
No kernel may reach another device: no remote copies, remote signals or barrier semaphores. Data moves between devices by JAX's collectives and lax.ppermute only.
A program may use at most 64 MiB of HBM per device.

v0:
```python
import functools
import math

import jax
import jax.numpy as jnp
from jax import lax
from jax.experimental import pallas as pl
from jax.experimental.pallas import tpu as pltpu
from jax.sharding import PartitionSpec as P


COLS = 512
ITERS = 6
W = 256
CHUNKS = COLS // W
TILES = W // 128
BELOW, ABOVE = 7, 9

coupling = 0.6
background = 0.25
TAN2 = math.tan(coupling) ** 2
SCALE = math.cos(coupling) ** 9 / math.tan(coupling)
TABLE_OF_STEP = (0, 0, 1, 2, 2, 3, 4, 4)


def passed_along(x, axis, by):
    devices = lax.axis_size(axis)
    return lax.ppermute(x, axis, [(i, (i + by) % devices) for i in range(devices)])


def turn(units):
    u = units * (1.0 / 32768.0)
    q = u * u
    half = math.pi / 2
    s = (-1) ** 5 * half**11 / math.factorial(11)
    for k in (4, 3, 2, 1, 0):
        s = s * q + (-1) ** k * half ** (2 * k + 1) / math.factorial(2 * k + 1)
    s = s * u
    c = half**12 / math.factorial(12)
    for k in (5, 4, 3, 2, 1, 0):
        c = c * q + (-1) ** k * half ** (2 * k) / math.factorial(2 * k)
    return 1.0 - 2.0 * s * s, 2.0 * s * c


def times(ar, ai, br, bi):
    return ar * br - ai * bi, ar * bi + ai * br


def in_hbm(x):
    return pltpu.with_memory_space_constraint(x, pltpu.HBM)


def pack_kernel(rows, incident, phase, *refs):
    outs, edge, sems, edge_sems = refs[:-3], refs[-3], refs[-2], refs[-1]
    sides = ((rows - BELOW, BELOW), (0, ABOVE))
    edges = [
        pltpu.make_async_copy(
            phase.at[:, first * COLS : (first + count) * COLS], edge.at[side, :, 0 : count * COLS], edge_sems.at[side]
        )
        for side, (first, count) in enumerate(sides)
    ]
    for c in edges:
        c.start()
    copies = []
    for chunk in range(CHUNKS):
        for side, (first, count) in enumerate(sides):
            out = outs[2 * chunk + side]
            for i in range(count):
                at = (first + i) * COLS + chunk * W
                for part in range(2):
                    copies.append(
                        pltpu.make_async_copy(
                            incident.at[part, :, at : at + W],
                            out.at[16 * part : 16 * part + 16, i * W : i * W + W],
                            sems.at[chunk, side, i, part],
                        )
                    )
                    copies[-1].start()
    for c in edges:
        c.wait()
    for chunk in range(CHUNKS):
        for side, (first, count) in enumerate(sides):
            out = outs[2 * chunk + side]
            for t in range(TILES):
                at = count * W + t * 128
                out[:, at : at + 128] = jnp.zeros((32, 128), jnp.float32)
                for i in range(count):
                    lane = i * COLS + chunk * W + t * 128
                    out[3 * i : 3 * i + 3, at : at + 128] = edge[side, :, lane : lane + 128].astype(jnp.float32)
    for c in copies:
        c.wait()


def pack(incident, phase):
    rows = incident.shape[2] // COLS
    widths = [BELOW * W + TILES * 128, ABOVE * W + TILES * 128] * CHUNKS
    return pl.pallas_call(
        functools.partial(pack_kernel, rows),
        out_shape=tuple(jax.ShapeDtypeStruct((32, w), jnp.float32) for w in widths),
        in_specs=[pl.BlockSpec(memory_space=pl.ANY)] * 2,
        out_specs=(pl.BlockSpec(memory_space=pltpu.VMEM),) * len(widths),
        scratch_shapes=[
            pltpu.VMEM((2, 3, ABOVE * COLS), jnp.int32),
            pltpu.SemaphoreType.DMA((CHUNKS, 2, ABOVE, 2)),
            pltpu.SemaphoreType.DMA((2,)),
        ],
        compiler_params=pltpu.CompilerParams(vmem_limit_bytes=8 * 1024 * 1024),
        cost_estimate=pl.CostEstimate(flops=0, bytes_accessed=2 * 1024 * 1024, transcendentals=0),
        name="pack",
    )(in_hbm(incident), in_hbm(phase))


PARTS = {
    "inner": ((0, 48),),
    "border": ((-8, 8), (47, 10)),
    "whole": ((-7, 64),),
}
OWN_ROWS = {"inner": ((0, 64),), "border": ((0, 16), (47, 64)), "whole": ((0, 64),)}
OWN_PHASES = {"inner": ((0, 64),), "border": ((0, 16), (40, 64)), "whole": ((0, 64),)}
TABLE_ROWS = {"inner": ((1, 9),), "border": ((0, 3), (6, 11)), "whole": ((0, 11),)}


def advance_gauge(gauge_in, gauge):
    step = gauge_in[8, 0], gauge_in[8, 1]
    strands = []
    for k in range(8):
        strands += [gauge_in[k, 0], gauge_in[k, 1]]
        gauge[k, 0] = strands[-2]
        gauge[k, 1] = strands[-1]

    def advance(i, strands):
        ahead = []
        for k in range(8):
            gr, gi = times(strands[2 * k], strands[2 * k + 1], *step)
            gauge[8 * i + 8 + k, 0] = gr
            gauge[8 * i + 8 + k, 1] = gi
            ahead += [gr, gi]
        return tuple(ahead)

    lax.fori_loop(0, 10, advance, tuple(strands))


def sweep_kernel(mode, chunk, incident, phase, gauge_in, *refs):
    below = above = inner_inten = stage = None
    if mode != "inner":
        below, above, refs = refs[0], refs[1], refs[2:]
    if mode == "border":
        inner_inten, refs = refs[0], refs[1:]
    raw_out, inten_out, last_out, own, wave, phases, tab, last, gauge, raw, stage, sems = refs
    arrivals = [
        pltpu.make_async_copy(incident.at[:, :, lo * COLS : hi * COLS], own.at[:, :, lo * COLS : hi * COLS], sems.at[k])
        for k, (lo, hi) in enumerate(OWN_ROWS[mode])
    ]
    for c in arrivals:
        c.start()
    advance_gauge(gauge_in, gauge)

    for t in range(TILES):
        for lo, hi in OWN_PHASES[mode]:
            for r in range(lo, hi):
                lane = r * COLS + chunk * W + t * 128
                units = phase[:, lane : lane + 128].astype(jnp.float32)
                for b in range(3):
                    phases[b, t, r + 8 : r + 9, :] = units[b : b + 1]
        if mode != "inner":
            for ref, count, first in ((below, BELOW, 1), (above, ABOVE, 72)):
                lanes = slice(count * W + t * 128, count * W + t * 128 + 128)
                for i in range(count):
                    for b in range(3):
                        phases[b, t, first + i : first + i + 1, :] = ref[3 * i + b : 3 * i + b + 1, lanes]

    top_row = lax.broadcasted_iota(jnp.int32, (8, 128), 0) == 0

    def tables(j, carried):
        at = pl.multiple_of(8 * j, 8)
        rolled = []
        for t in range(TILES):
            here, before = [], []
            for b in range(3):
                here.append(turn(phases[b, t, pl.ds(at, 8), :]))
                pair = []
                for q in range(2):
                    r = pltpu.roll(here[b][q], 1, 0)
                    pair.append(jnp.where(top_row, carried[(t * 3 + b) * 2 + q], r))
                    rolled.append(r)
                before.append(pair)
            for k, (a, b) in enumerate(((0, 0), (0, 1), (1, 1), (1, 2), (2, 2))):
                br, bi = before[b]
                ar, ai = here[a]
                tab[k, 0, t, pl.ds(at, 8), :] = ar * br + ai * bi
                tab[k, 1, t, pl.ds(at, 8), :] = ai * br - ar * bi
            last[0, t, pl.ds(at, 8), :] = SCALE * here[2][1]
            last[1, t, pl.ds(at, 8), :] = -SCALE * here[2][0]
        return tuple(rolled)

    for lo, hi in TABLE_ROWS[mode]:
        lax.fori_loop(lo, hi, tables, (jnp.zeros((8, 128), jnp.float32),) * (6 * TILES))
    departures = [pltpu.make_async_copy(last, last_out, sems.at[2])]
    departures[0].start()

    def regauge(row, at, re_of, im_of):
        er, ei = gauge[row + 10, 0], gauge[row + 10, 1]
        for t in range(TILES):
            tr, ti = times(re_of(t), im_of(t), er, ei)
            wave[at, 0, :, t * 128 : t * 128 + 128] = tr
            wave[at, 1, :, t * 128 : t * 128 + 128] = ti

    def packet(r0, low, place, tile, state, steps):
        lanes = pl.ds(pl.multiple_of(tile * 128, 128), 128)
        tr = wave[r0 - low, 0, :, lanes]
        ti = wave[r0 - low, 1, :, lanes]
        after = []
        for n in range(steps):
            if n == 0:
                nr, ni = -TAN2 * tr, -TAN2 * ti
            else:
                dr, di = state[2 * n - 2], state[2 * n - 1]
                nr, ni = dr - TAN2 * tr, di - TAN2 * ti
                if n < steps - 1:
                    tr, ti = tr + dr, ti + di
            if n < 8:
                k = TABLE_OF_STEP[n]
                hr = tab[k, 0, tile, pl.ds(r0 + n + 8, 1), :]
                hi = tab[k, 1, tile, pl.ds(r0 + n + 8, 1), :]
                after += times(nr, ni, hr, hi)
        if steps == 9:
            raw[tile, place + r0 - low, 0] = nr
            raw[tile, place + r0 - low, 1] = ni
            inten = SCALE * SCALE * (nr * nr + ni * ni)
            if mode == "inner":
                inten_out[r0 - low, :, lanes] = inten
            elif mode == "border":
                stage[place + r0 - low, :, lanes] = inten
            else:
                row = r0 + 7
                off = pl.multiple_of((row % 4) * W + tile * 128, 128)
                inten_out[row // 4, :, pl.ds(off, 128)] = inten
        return tuple(after)

    for c in arrivals:
        c.wait()
    place = 0
    for low, count in PARTS[mode]:
        high = low + count + 15
        if low < 0:
            for i in range(BELOW):
                lanes = lambda t, i=i: slice(i * W + t * 128, i * W + t * 128 + 128)
                regauge(i - BELOW, i - BELOW - low, lambda t: below[0:16, lanes(t)], lambda t: below[16:32, lanes(t)])
        if high > 64:
            for i in range(ABOVE):
                lanes = lambda t, i=i: slice(i * W + t * 128, i * W + t * 128 + 128)
                regauge(64 + i, 64 + i - low, lambda t: above[0:16, lanes(t)], lambda t: above[16:32, lanes(t)])

        def own_row(row, low=low):
            lanes = lambda t: pl.ds(pl.multiple_of(row * COLS + chunk * W + t * 128, 128), 128)
            regauge(row, row - low, lambda t: own[0, :, lanes(t)], lambda t: own[1, :, lanes(t)])

        first, end = max(low, 0), min(high, 63) + 1
        fours = (end - first) // 4

        @pl.loop(0, fours)
        def _(j, first=first, own_row=own_row):
            for k in range(4):
                own_row(first + 4 * j + k)

        for row in range(first + 4 * fours, end):
            own_row(row)

        @pl.loop(0, TILES)
        def _(tile, low=low, high=high, count=count, place=place):
            @pl.loop(0, 2)
            def _(odd):
                top = high - odd
                state = ()
                for i in range(8):
                    state = packet(top - 2 * i, low, place, tile, state, i + 1)
                group = 5 if count == 10 else 4

                def several(j, state):
                    for i in range(group):
                        state = packet(top - 16 - 2 * group * j - 2 * i, low, place, tile, state, 9)
                    return state

                lax.fori_loop(0, count // 2 // group, several, state)

            if mode != "border":
                pltpu.make_async_copy(raw.at[tile], raw_out.at[tile], sems.at[3 + tile]).start()

        place += count
    if mode == "border":
        for tile in range(TILES):
            pltpu.make_async_copy(raw.at[tile], raw_out.at[tile], sems.at[3 + tile]).start()
        for row in range(64):
            if row < 7:
                value = stage[row + 1]
            elif row < 55:
                value = inner_inten[row - 7]
            else:
                value = stage[row - 46]
            inten_out[row // 4, :, (row % 4) * W : (row % 4) * W + W] = value
    departures[0].wait()
    for tile in range(TILES):
        pltpu.make_async_copy(raw.at[tile], raw_out.at[tile], sems.at[3 + tile]).wait()


def whole_block(shape):
    return pl.BlockSpec(shape, lambda i: (0,) * len(shape))


def sweep(mode, incident, phase, gauge, chunk, *more):
    total = sum(count for _, count in PARTS[mode])
    tall = max(count for _, count in PARTS[mode]) + 16
    shapes = ((TILES, total, 2, 16, 128), (48, 16, W) if mode == "inner" else (16, 16, 4 * W), (2, TILES, 88, 128))
    vmem, hbm = pl.BlockSpec(memory_space=pltpu.VMEM), pl.BlockSpec(memory_space=pltpu.HBM)
    return pl.pallas_call(
        functools.partial(sweep_kernel, mode, chunk),
        out_shape=(
            pltpu.HBM(shapes[0], jnp.float32),
            jax.ShapeDtypeStruct(shapes[1], jnp.float32),
            pltpu.HBM(shapes[2], jnp.float32),
        ),
        in_specs=[pl.BlockSpec(memory_space=pl.ANY)] + [vmem] * (2 + len(more)),
        out_specs=(hbm, vmem, hbm),
        scratch_shapes=[
            pltpu.VMEM(incident.shape, jnp.float32),
            pltpu.VMEM((tall, 2, 16, W), jnp.float32),
            pltpu.VMEM((3, TILES, 88, 128), jnp.float32),
            pltpu.VMEM((5, 2, TILES, 88, 128), jnp.float32),
            pltpu.VMEM((2, TILES, 88, 128), jnp.float32),
            pltpu.VMEM((88, 2, 16, 128), jnp.float32),
            pltpu.VMEM((TILES, total, 2, 16, 128), jnp.float32),
            pltpu.VMEM((18, 16, W), jnp.float32),
            pltpu.SemaphoreType.DMA((3 + TILES,)),
        ],
        compiler_params=pltpu.CompilerParams(vmem_limit_bytes=24 * 1024 * 1024),
        cost_estimate=pl.CostEstimate(flops=total * 16 * W * 120, bytes_accessed=8 * 1024 * 1024, transcendentals=0),
        name="sweep",
    )(in_hbm(incident), phase, gauge, *more)


def merge_kernel(gauge_in, inner, border, whole, last_inner, last_border, last_whole, out, gauge):
    advance_gauge(gauge_in, gauge)

    def put(row, chunk, ref, at, last):
        er, ei = gauge[row + 1, 0], gauge[row + 1, 1]
        for t in range(TILES):
            fr, fi = (last[q, t, pl.ds(row + 9, 1), :] for q in range(2))
            tr, ti = times(ref[t, at, 0], ref[t, at, 1], fr, fi)
            off = pl.multiple_of(row * COLS + chunk * W + t * 128, 128)
            out[0, :, pl.ds(off, 128)] = tr * er + ti * ei
            out[1, :, pl.ds(off, 128)] = ti * er - tr * ei

    @pl.loop(0, 24)
    def _(j):
        for k in range(2):
            put(2 * j + k + 7, 0, inner, 2 * j + k, last_inner)

    for row in range(7):
        put(row, 0, border, row + 1, last_border)
    for row in range(55, 64):
        put(row, 0, border, row - 46, last_border)

    @pl.loop(0, 32)
    def _(j):
        for k in range(2):
            put(2 * j + k, 1, whole, 2 * j + k, last_whole)


def merge(gauge, raws, lasts, span):
    return pl.pallas_call(
        merge_kernel,
        grid=(1,),
        out_shape=jax.ShapeDtypeStruct((2, 16, span), jnp.float32),
        in_specs=[whole_block(x.shape) for x in (gauge, *raws, *lasts)],
        out_specs=whole_block((2, 16, span)),
        scratch_shapes=[pltpu.VMEM((88, 2, 16, 128), jnp.float32)],
        cost_estimate=pl.CostEstimate(flops=0, bytes_accessed=8 * 1024 * 1024, transcendentals=0),
        name="merge",
    )(gauge, *raws, *lasts)


def place_kernel(chunk, block, *refs):
    out, sems = refs[-2:]
    copies = []
    for b in range(16):
        for r in range(4):
            at = (4 * b + r) * COLS + chunk * W
            copies.append(pltpu.make_async_copy(block.at[b, :, r * W : r * W + W], out.at[:, at : at + W], sems.at[b, r]))
            copies[-1].start()
    for c in copies:
        c.wait()


def place(block, chunk, span, onto=None):
    hbm = pl.BlockSpec(memory_space=pl.ANY)
    ops = [block] if onto is None else [block, onto]
    return pl.pallas_call(
        functools.partial(place_kernel, chunk),
        out_shape=jax.ShapeDtypeStruct((16, span), jnp.float32),
        in_specs=[pl.BlockSpec(memory_space=pltpu.VMEM)] + [hbm] * (len(ops) - 1),
        out_specs=hbm,
        scratch_shapes=[pltpu.SemaphoreType.DMA((16, 4))],
        input_output_aliases={} if onto is None else {1: 0},
        compiler_params=pltpu.CompilerParams(vmem_limit_bytes=4 * 1024 * 1024),
        cost_estimate=pl.CostEstimate(flops=0, bytes_accessed=4 * 1024 * 1024, transcendentals=0),
        name="place",
    )(*ops)


def deconvolve(estimate, response, scaled, measured):
    for _ in range(ITERS):
        blurred = jnp.dot(response, estimate, precision=lax.Precision.HIGH, preferred_element_type=jnp.float32) + background
        projected = lax.dot_general(
            scaled,
            measured / blurred,
            (((0,), (0,)), ((), ())),
            precision=lax.Precision.HIGH,
            preferred_element_type=jnp.float32,
        )
        estimate = estimate * projected
    return estimate


def exchange(x):
    return lax.all_to_all(x, "ang", split_axis=0, concat_axis=0, tiled=True)


def on_device(incident, detuning, phase_table, response, counts):
    span = incident.shape[2]
    edges = pack(incident, phase_table)
    below, above = [], []
    for chunk in range(CHUNKS):
        below.append(passed_along(edges[2 * chunk], "lat", 1))
        above.append(passed_along(edges[2 * chunk + 1], "lat", -1))
    angle = -0.5 * detuning[None, :] * jnp.array([-10.0, -9.0, -8.0, -7.0, -6.0, -5.0, -4.0, -3.0, 8.0], jnp.float32)[:, None]
    gauge = jnp.stack([jnp.cos(angle), jnp.sin(angle)], axis=1)
    gauge = jnp.broadcast_to(gauge[..., None], gauge.shape + (128,))

    column_sums = jnp.sum(response, axis=0)
    scaled = response / column_sums[None, :]
    measured = [
        jnp.concatenate([counts[:, r * COLS + c * W : r * COLS + c * W + W] for r in range(4)], axis=1).astype(jnp.float32)
        for c in range(CHUNKS)
    ]

    raw_inner, inten_inner, last_inner = sweep("inner", incident, phase_table, gauge, 0)
    raw_border, inten0, last_border = sweep("border", incident, phase_table, gauge, 0, below[0], above[0], inten_inner)
    there0 = exchange(inten0)
    raw_whole, inten1, last_whole = sweep("whole", incident, phase_table, gauge, 1, below[1], above[1])
    there1 = exchange(inten1)
    estimate0 = deconvolve(there0.reshape(256, 4 * W), response, scaled, measured[0])
    back0 = exchange(estimate0.reshape(16, 16, 4 * W))
    there1, estimate0 = lax.optimization_barrier((there1, estimate0))
    estimate1 = deconvolve(there1.reshape(256, 4 * W), response, scaled, measured[1])
    back1 = exchange(estimate1.reshape(16, 16, 4 * W))
    exit_field = merge(gauge, (raw_inner, raw_border, raw_whole), (last_inner, last_border, last_whole), span)
    result = place(back0, 0, span)
    result = place(back1, 1, span, result)
    return exit_field, result


def solution(mesh):
    return jax.shard_map(
        on_device,
        mesh=mesh,
        in_specs=(P(None, "ang", "lat"), P("ang"), P(None, "lat"), P(), P(None, ("lat", "ang"))),
        out_specs=(P(None, "ang", "lat"), P("ang", "lat")),
        check_vma=False,
    )
```

profile of v0, /device:TPU:24, one launch (start us, length us, event | category | flops | bytes accessed | tf_op | source)
XLA Modules:
  0.0 130.5 jit_solution(2890017142957849470)
XLA Ops:
  0.6 0.0 copy-start.10
  0.6 0.0 copy-start
  0.7 0.0 copy-start.11
  0.7 2.2 %pack.1 = (f32[32,2048]{1,0:T(8,128)S(1)}, f32[32,2560]{1,0:T(8,128)S(1)}, f32[32,2048]{1,0:T(8,128)S(1)}, f32[32,2560]{1,0:T(8,128)S(1)}) custom-call(f32[2,16,32768]{2,1,0:T(8,128)} %incident.7, s32[3,32768]{1,0:T(4,128)} %phase.7), custom_call_target="tpu_custom_call" | custom-call | bytes 2097152 | tf_op jit(solution)/shard_map/pack/pallas_call | solution.py:97
  2.8 0.8 collective-permute-start.1
  3.7 4.9 %collective-permute-start = (f32[32,2048]{1,0:T(8,128)S(1)}, f32[32,2048]{1,0:T(8,128)S(1)}, u32[]{:S(2)}, u32[]{:S(2)}) collective-permute-start(f32[32,2048]{1,0:T(8,128)S(1)} %get-tuple-element.17), channel_id=1, source_target_pairs={{0,16},{16,32},{32,48},{48,64},{64,80},{80,96},{96,112},{112,0},{1... | collective-permute-start | bytes 786440 | tf_op jit(solution)/shard_map/ppermute | solution.py:28
  8.6 0.0 copy-done.11
  8.6 0.0 copy-done.10
  8.6 0.2 multiply_cosine_fusion
  8.8 0.1 broadcast_in_dim.2.gauge_in
  8.9 0.0 copy-done
  8.9 0.0 copy-start.1
  8.9 7.0 %sweep.3 = (f32[2,48,2,16,128]{4,3,2,1,0:T(8,128)}, f32[48,16,256]{2,1,0:T(8,128)S(1)}, f32[2,2,88,128]{3,2,1,0:T(8,128)}) custom-call(f32[2,16,32768]{2,1,0:T(8,128)} %incident.7, s32[3,32768]{1,0:T(4,128)S(1)} %copy-done, f32[9,2,16,128]{3,2,1,0:T(8,128)S(1)} %broadcast_in_dim.2.gauge_in), custom_call_target="tpu_custom_call" | custom-call | flops 23592960 | bytes 8388608 | tf_op jit(solution)/shard_map/sweep/pallas_call | solution.py:315
  15.9 0.0 collective-permute-done.refs_0_
  15.9 0.1 collective-permute-done.1.refs_1_
  16.0 5.4 %sweep.4 = (f32[2,18,2,16,128]{4,3,2,1,0:T(8,128)}, f32[16,16,1024]{2,1,0:T(8,128)}, f32[2,2,88,128]{3,2,1,0:T(8,128)}) custom-call(f32[2,16,32768]{2,1,0:T(8,128)} %incident.7, s32[3,32768]{1,0:T(4,128)S(1)} %copy-done, f32[9,2,16,128]{3,2,1,0:T(8,128)S(1)} %broadcast_in_dim.2.gauge_in, f32[32,2048]{1,0:T(8,128)S(1)} %collective-permute-done.refs_0_, ...), custom_call_target="tpu_custom_call" | custom-call | flops 8847360 | bytes 8388608 | tf_op jit(solution)/shard_map/sweep/pallas_call | solution.py:315
  21.4 0.0 copy-start.2
  21.4 6.5 %all-to-all-start.1 = ((f32[16,16,1024]{2,1,0:T(8,128)}), f32[16,16,1024]{2,1,0:T(8,128)S(1)}, u32[]{:S(2)}, u32[]{:S(2)}) async-start(f32[16,16,1024]{2,1,0:T(8,128)} %get-tuple-element.28), calls=%async_computation.1 | async-start | bytes 2097152 | tf_op jit(solution)/shard_map/all_to_all | solution.py:425
  27.9 0.1 collective-permute-start.3
  28.0 5.6 %collective-permute-start.2 = (f32[32,2048]{1,0:T(8,128)S(1)}, f32[32,2048]{1,0:T(8,128)S(1)}, u32[]{:S(2)}, u32[]{:S(2)}) collective-permute-start(f32[32,2048]{1,0:T(8,128)S(1)} %get-tuple-element.21), channel_id=1, source_target_pairs={{0,16},{16,32},{32,48},{48,64},{64,80},{80,96},{96,112},{112,0},{1... | collective-permute-start | bytes 786440 | tf_op jit(solution)/shard_map/ppermute | solution.py:28
  33.6 0.0 copy-done.2
  33.7 2.8 %fusion.24 = (s32[256,256]{1,0:T(8,128)S(1)}, s32[256,256]{1,0:T(8,128)}, s32[256,256]{1,0:T(8,128)}, s32[256,256]{1,0:T(8,128)}, s32[256,256]{1,0:T(8,128)}, /*...) fusion(s32[256,2048]{1,0:T(8,128)} %param.10), kind=kLoop, calls=%fused_computation.55 | loop fusion | bytes 4194304 | tf_op jit(solution)/shard_map/slice | solution.py:442
  36.5 9.4 %collective-permute-done.2.refs_0_ = f32[32,2048]{1,0:T(8,128)S(1)} collective-permute-done((f32[32,2048]{1,0:T(8,128)S(1)}, f32[32,2048]{1,0:T(8,128)S(1)}, u32[]{:S(2)}, u32[]{:S(2)}) %collective-permute-start.2) | collective-permute-done | bytes 262176 | tf_op jit(solution)/shard_map/ppermute | solution.py:28
  45.9 6.4 %collective-permute-done.3.refs_1_ = f32[32,2560]{1,0:T(8,128)S(1)} collective-permute-done((f32[32,2560]{1,0:T(8,128)S(1)}, f32[32,2560]{1,0:T(8,128)S(1)}, u32[]{:S(2)}, u32[]{:S(2)}) %collective-permute-start.3) | collective-permute-done | bytes 327712 | tf_op jit(solution)/shard_map/ppermute | solution.py:28
  52.3 0.0 copy-done.1
  52.3 8.9 %sweep.5 = (f32[2,64,2,16,128]{4,3,2,1,0:T(8,128)}, f32[16,16,1024]{2,1,0:T(8,128)}, f32[2,2,88,128]{3,2,1,0:T(8,128)}) custom-call(f32[2,16,32768]{2,1,0:T(8,128)} %incident.7, s32[3,32768]{1,0:T(4,128)S(1)} %copy-done, f32[9,2,16,128]{3,2,1,0:T(8,128)S(1)} %broadcast_in_dim.2.gauge_in, f32[32,2048]{1,0:T(8,128)S(1)} %collective-permute-done.2.refs_0_, ...), custom_call_target="tpu_custom_call" | custom-call | flops 31457280 | bytes 8388608 | tf_op jit(solution)/shard_map/sweep/pallas_call | solution.py:315
  61.2 0.0 copy-start.6
  61.2 0.0 copy-start.7
  61.2 0.0 all-to-all-done.1
  61.2 5.1 %all-to-all-start = ((f32[16,16,1024]{2,1,0:T(8,128)}), f32[16,16,1024]{2,1,0:T(8,128)S(1)}, u32[]{:S(2)}, u32[]{:S(2)}) async-start(f32[16,16,1024]{2,1,0:T(8,128)} %get-tuple-element.27), calls=%async_computation | async-start | bytes 2097152 | tf_op jit(solution)/shard_map/all_to_all | solution.py:425
  66.4 1.7 %fusion.23 = f32[256,1024]{1,0:T(8,128)S(1)} fusion(f32[256,1024]{1,0:T(8,128)S(1)} %bitcast.88, f32[256,256]{1,0:T(8,128)S(1)} %copy-done.2, s32[256,256]{1,0:T(8,128)S(1)} %copy-done.6, s32[256,256]{1,0:T(8,128)S(1)} %copy-done.7, s32[256,256]{1,0:T(8,128)S(1)} %copy-done.8, s32[256,256]{1,0:T(8,128)} %get-tuple-element.35), kind=kOutput, calls=%fused_computation.47 | convolution fusion | flops 404226048 | bytes 3407872 | tf_op jit(solution)/shard_map/dot_general | solution.py:412
  68.0 0.0 copy-start.9
  68.0 0.7 convolution_multiply_fusion.11
  68.7 0.3 copy-done.9
  69.0 0.7 fusion.21
  69.7 0.7 convolution_multiply_fusion.10
  70.4 0.7 fusion.19
  71.1 0.7 convolution_multiply_fusion.9
  71.7 0.7 fusion.17
  72.4 0.7 convolution_multiply_fusion.8
  73.1 0.7 fusion.15
  73.8 0.7 convolution_multiply_fusion.7
  74.5 0.7 fusion.13
  75.2 1.6 %convolution_multiply_fusion.6 = f32[256,1024]{1,0:T(8,128)} fusion(f32[256,1024]{1,0:T(8,128)S(1)} %convolution_multiply_fusion.7, f32[256,1024]{1,0:T(8,128)S(1)} %fusion.13, f32[256,256]{1,0:T(8,128)S(1)} %copy-done.2, f32[256]{0:T(256)S(1)} %reduce_sum.9), kind=kOutput, calls=%fused_computation.24 | convolution fusion | flops 402980864 | bytes 3408896 | tf_op jit(solution)/shard_map/dot_general | solution.py:413
  76.9 5.8 %all-to-all-done = f32[16,16,1024]{2,1,0:T(8,128)S(1)} async-done(((f32[16,16,1024]{2,1,0:T(8,128)}), f32[16,16,1024]{2,1,0:T(8,128)S(1)}, u32[]{:S(2)}, u32[]{:S(2)}) %all-to-all-start) | async-done | bytes 1048608 | tf_op jit(solution)/shard_map/all_to_all | solution.py:425
  82.7 0.7 fusion.11
  83.4 0.7 convolution_multiply_fusion.5
  84.1 0.7 fusion.9
  84.8 0.7 convolution_multiply_fusion.4
  85.5 0.7 fusion.7
  86.2 0.9 convolution_multiply_fusion.3
  87.1 0.7 fusion.5
  87.8 0.7 convolution_multiply_fusion.2
  88.4 3.7 %all-to-all-start.3 = ((f32[16,16,1024]{2,1,0:T(8,128)}), f32[16,16,1024]{2,1,0:T(8,128)S(1)}, u32[]{:S(2)}, u32[]{:S(2)}) async-start(f32[16,16,1024]{2,1,0:T(8,128)} %bitcast.15), calls=%async_computation.3 | async-start | bytes 2097152 | tf_op jit(solution)/shard_map/all_to_all | solution.py:425
  92.1 0.7 fusion.3
  92.8 0.7 convolution_multiply_fusion.1
  93.5 0.7 fusion.1
  94.2 1.6 %convolution_multiply_fusion = f32[256,1024]{1,0:T(8,128)} fusion(f32[256,1024]{1,0:T(8,128)S(1)} %convolution_multiply_fusion.1, f32[256,1024]{1,0:T(8,128)S(1)} %fusion.1, f32[256,256]{1,0:T(8,128)S(1)} %copy-done.2, f32[256]{0:T(256)S(1)} %reduce_sum.9), kind=kOutput, calls=%fused_computation | convolution fusion | flops 402980864 | bytes 3408896 | tf_op jit(solution)/shard_map/dot_general | solution.py:413
  95.8 12.8 %all-to-all-done.3.block = f32[16,16,1024]{2,1,0:T(8,128)S(1)} async-done(((f32[16,16,1024]{2,1,0:T(8,128)}), f32[16,16,1024]{2,1,0:T(8,128)S(1)}, u32[]{:S(2)}, u32[]{:S(2)}) %all-to-all-start.3) | async-done | bytes 1048608 | tf_op jit(solution)/shard_map/all_to_all | solution.py:425
  108.6 3.7 %all-to-all-start.2 = ((f32[16,16,1024]{2,1,0:T(8,128)}), f32[16,16,1024]{2,1,0:T(8,128)S(1)}, u32[]{:S(2)}, u32[]{:S(2)}) async-start(f32[16,16,1024]{2,1,0:T(8,128)} %bitcast.14), calls=%async_computation.2 | async-start | bytes 2097152 | tf_op jit(solution)/shard_map/all_to_all | solution.py:425
  112.3 5.7 %merge.1 = f32[2,16,32768]{2,1,0:T(8,128)} custom-call(f32[9,2,16,128]{3,2,1,0:T(8,128)} %copy-done.1, f32[2,48,2,16,128]{4,3,2,1,0:T(8,128)} %get-tuple-element.16.inner, f32[2,18,2,16,128]{4,3,2,1,0:T(8,128)} %get-tuple-element.20.border, f32[2,64,2,16,128]{4,3,2,1,0:T(8,128)} %get-tuple-element.23.whole, f32[2,2,88,128]{3,2,1,0:T(8,128)} %get-tuple-element.24.last_inner, ...), custom_call_target="tpu_custom_call" | custom-call | bytes 8388608 | tf_op jit(solution)/shard_map/merge/pallas_call | solution.py:370
  118.0 1.5 %place.2.refs_0_ = f32[16,32768]{1,0:T(8,128)} custom-call(f32[16,16,1024]{2,1,0:T(8,128)S(1)} %all-to-all-done.3.block), custom_call_target="tpu_custom_call" | custom-call | bytes 4194304 | tf_op jit(solution)/shard_map/place/pallas_call | solution.py:397
  119.5 9.3 %all-to-all-done.2.block = f32[16,16,1024]{2,1,0:T(8,128)S(1)} async-done(((f32[16,16,1024]{2,1,0:T(8,128)}), f32[16,16,1024]{2,1,0:T(8,128)S(1)}, u32[]{:S(2)}, u32[]{:S(2)}) %all-to-all-start.2) | async-done | bytes 1048608 | tf_op jit(solution)/shard_map/all_to_all | solution.py:425
  128.8 1.5 %place.3 = f32[16,32768]{1,0:T(8,128)} custom-call(f32[16,16,1024]{2,1,0:T(8,128)S(1)} %all-to-all-done.2.block, f32[16,32768]{1,0:T(8,128)} %place.2.refs_0_), custom_call_target="tpu_custom_call", output_to_operand_aliasing={{}: (1, {})} | custom-call | bytes 4194304 | tf_op jit(solution)/shard_map/place/pallas_call | solution.py:397
  (13 shorter events, 0.1 us)
Async XLA Ops:
  0.6 7.9 %copy-start.10 = (f32[9]{0:T(128)S(1)}, f32[9]{0:T(128)}, u32[]{:S(2)}) copy-start(f32[9]{0:T(128)} %constant.8.clone) | copy-start | bytes 112
  0.6 8.3 %copy-start = (s32[3,32768]{1,0:T(4,128)S(1)}, s32[3,32768]{1,0:T(4,128)}, u32[]{:S(2)}) copy-start(s32[3,32768]{1,0:T(4,128)} %phase.7) | copy-start | bytes 1179652
  0.7 7.9 %copy-start.11 = (f32[16]{0:T(128)S(1)}, f32[16]{0:T(128)}, u32[]{:S(2)}) copy-start(f32[16]{0:T(128)} %param.7) | copy-start | bytes 196
  2.8 13.1 %collective-permute-start.1 = (f32[32,2560]{1,0:T(8,128)S(1)}, f32[32,2560]{1,0:T(8,128)S(1)}, u32[]{:S(2)}, u32[]{:S(2)}) collective-permute-start(f32[32,2560]{1,0:T(8,128)S(1)} %get-tuple-element.18), channel_id=1, source_target_pairs={{0,112},{16,0},{32,16},{48,32},{64,48},{80,64},{96,80},{112,96},{1... | collective-permute-start | bytes 983048 | tf_op jit(solution)/shard_map/ppermute | solution.py:28
  3.7 12.2 %collective-permute-start = (f32[32,2048]{1,0:T(8,128)S(1)}, f32[32,2048]{1,0:T(8,128)S(1)}, u32[]{:S(2)}, u32[]{:S(2)}) collective-permute-start(f32[32,2048]{1,0:T(8,128)S(1)} %get-tuple-element.17), channel_id=1, source_target_pairs={{0,16},{16,32},{32,48},{48,64},{64,80},{80,96},{96,112},{112,0},{1... | collective-permute-start | bytes 786440 | tf_op jit(solution)/shard_map/ppermute | solution.py:28
  8.9 43.4 %copy-start.1 = (f32[9,2,16,128]{3,2,1,0:T(8,128)}, f32[9,2,16,128]{3,2,1,0:T(8,128)S(1)}, u32[]{:S(2)}) copy-start(f32[9,2,16,128]{3,2,1,0:T(8,128)S(1)} %broadcast_in_dim.2.gauge_in) | copy-start | bytes 442372
  21.4 12.2 %copy-start.2 = (f32[256,256]{1,0:T(8,128)S(1)}, f32[256,256]{1,0:T(8,128)}, u32[]{:S(2)}) copy-start(f32[256,256]{1,0:T(8,128)} %param.9) | copy-start | bytes 786436
  21.4 39.8 %all-to-all-start.1 = ((f32[16,16,1024]{2,1,0:T(8,128)}), f32[16,16,1024]{2,1,0:T(8,128)S(1)}, u32[]{:S(2)}, u32[]{:S(2)}) async-start(f32[16,16,1024]{2,1,0:T(8,128)} %get-tuple-element.28), calls=%async_computation.1 | async-start | bytes 2097152 | tf_op jit(solution)/shard_map/all_to_all | solution.py:425
  27.9 24.4 %collective-permute-start.3 = (f32[32,2560]{1,0:T(8,128)S(1)}, f32[32,2560]{1,0:T(8,128)S(1)}, u32[]{:S(2)}, u32[]{:S(2)}) collective-permute-start(f32[32,2560]{1,0:T(8,128)S(1)} %get-tuple-element.22), channel_id=1, source_target_pairs={{0,112},{16,0},{32,16},{48,32},{64,48},{80,64},{96,80},{112,96},{1... | collective-permute-start | bytes 983048 | tf_op jit(solution)/shard_map/ppermute | solution.py:28
  28.0 17.9 %collective-permute-start.2 = (f32[32,2048]{1,0:T(8,128)S(1)}, f32[32,2048]{1,0:T(8,128)S(1)}, u32[]{:S(2)}, u32[]{:S(2)}) collective-permute-start(f32[32,2048]{1,0:T(8,128)S(1)} %get-tuple-element.21), channel_id=1, source_target_pairs={{0,16},{16,32},{32,48},{48,64},{64,80},{80,96},{96,112},{112,0},{1... | collective-permute-start | bytes 786440 | tf_op jit(solution)/shard_map/ppermute | solution.py:28
  61.2 5.1 %copy-start.6 = (s32[256,256]{1,0:T(8,128)S(1)}, s32[256,256]{1,0:T(8,128)}, u32[]{:S(2)}) copy-start(s32[256,256]{1,0:T(8,128)} %get-tuple-element.32) | copy-start | bytes 786436
  61.2 5.1 %copy-start.7 = (s32[256,256]{1,0:T(8,128)S(1)}, s32[256,256]{1,0:T(8,128)}, u32[]{:S(2)}) copy-start(s32[256,256]{1,0:T(8,128)} %get-tuple-element.33) | copy-start | bytes 786436
  61.2 5.1 %copy-start.8 = (s32[256,256]{1,0:T(8,128)S(1)}, s32[256,256]{1,0:T(8,128)}, u32[]{:S(2)}) copy-start(s32[256,256]{1,0:T(8,128)} %get-tuple-element.34) | copy-start | bytes 786436
  61.2 21.5 %all-to-all-start = ((f32[16,16,1024]{2,1,0:T(8,128)}), f32[16,16,1024]{2,1,0:T(8,128)S(1)}, u32[]{:S(2)}, u32[]{:S(2)}) async-start(f32[16,16,1024]{2,1,0:T(8,128)} %get-tuple-element.27), calls=%async_computation | async-start | bytes 2097152 | tf_op jit(solution)/shard_map/all_to_all | solution.py:425
  68.0 1.0 copy-start.9
  75.2 7.5 %copy-start.3 = (s32[256,256]{1,0:T(8,128)S(1)}, s32[256,256]{1,0:T(8,128)}, u32[]{:S(2)}) copy-start(s32[256,256]{1,0:T(8,128)} %get-tuple-element.31) | copy-start | bytes 786436
  75.2 7.5 %copy-start.4 = (s32[256,256]{1,0:T(8,128)S(1)}, s32[256,256]{1,0:T(8,128)}, u32[]{:S(2)}) copy-start(s32[256,256]{1,0:T(8,128)} %get-tuple-element.36) | copy-start | bytes 786436
  75.2 7.5 %copy-start.5 = (s32[256,256]{1,0:T(8,128)S(1)}, s32[256,256]{1,0:T(8,128)}, u32[]{:S(2)}) copy-start(s32[256,256]{1,0:T(8,128)} %get-tuple-element.37) | copy-start | bytes 786436
  88.4 20.2 %all-to-all-start.3 = ((f32[16,16,1024]{2,1,0:T(8,128)}), f32[16,16,1024]{2,1,0:T(8,128)S(1)}, u32[]{:S(2)}, u32[]{:S(2)}) async-start(f32[16,16,1024]{2,1,0:T(8,128)} %bitcast.15), calls=%async_computation.3 | async-start | bytes 2097152 | tf_op jit(solution)/shard_map/all_to_all | solution.py:425
  108.6 20.2 %all-to-all-start.2 = ((f32[16,16,1024]{2,1,0:T(8,128)}), f32[16,16,1024]{2,1,0:T(8,128)S(1)}, u32[]{:S(2)}, u32[]{:S(2)}) async-start(f32[16,16,1024]{2,1,0:T(8,128)} %bitcast.14), calls=%async_computation.2 | async-start | bytes 2097152 | tf_op jit(solution)/shard_map/all_to_all | solution.py:425
where the time goes:
time: 131 us; the launch traced here: 130 us
  waiting for transfers between devices  43.7 us (33%)
  Pallas kernels  32.2 us (25%)
  starting transfers between devices  30.3 us (23%)
  matrix products  19.5 us (15%)
  local copies, waits for them, and re-layouts  3.24 us (2%)
    all_to_all x4, waiting for transfers between devices, exchange(): return lax.all_to_all(x, 'ang', split_axis=0, concat_axis=0, tiled=True)  27.9 us
    pallas_call x3, Pallas kernels, sweep(): pl.pallas_call(functools.partial(sweep_kernel, mode, chunk), out_shape=(p...  21.3 us
    all_to_all x4, starting transfers between devices, exchange(): return lax.all_to_all(x, 'ang', split_axis=0, concat_axis=0, tiled=True)  18.9 us
    ppermute x4, waiting for transfers between devices, passed_along(): lax.ppermute(x, axis, [(i, (i + by) % devices) for i in range(devices)])  15.9 us
    ppermute x4, starting transfers between devices, passed_along(): lax.ppermute(x, axis, [(i, (i + by) % devices) for i in range(devices)])  11.4 us
    dot_general x12, matrix products, deconvolve(): lax.dot_general(scaled, measured / blurred, (((0,), (0,)), ((), ())), pre...  10 us
    dot_general x12, matrix products, deconvolve(): jnp.dot(response, estimate, precision=lax.Precision.HIGH, preferred_eleme...  9.44 us
    pallas_call x1, Pallas kernels, merge(): pl.pallas_call(merge_kernel, grid=(1,), out_shape=jax.ShapeDtypeStruct((2...  5.73 us
  transfers between devices with their start and end apart: 8, of which 6 were waited for; matrix products, arithmetic and copies ran while one was open for 13% of the time, Pallas kernels for 18%

commit v1 on v0

--- a/solution.py
+++ b/solution.py
@@ -50,8 +50,9 @@
     return pltpu.with_memory_space_constraint(x, pltpu.HBM)
 
 
-def pack_kernel(rows, incident, phase, *refs):
+def pack_kernel(incident, phase, *refs):
     outs, edge, sems, edge_sems = refs[:-3], refs[-3], refs[-2], refs[-1]
+    rows = incident.shape[2] // COLS
     sides = ((rows - BELOW, BELOW), (0, ABOVE))
     edges = [
         pltpu.make_async_copy(
@@ -64,14 +65,13 @@
     copies = []
     for chunk in range(CHUNKS):
         for side, (first, count) in enumerate(sides):
-            out = outs[2 * chunk + side]
             for i in range(count):
                 at = (first + i) * COLS + chunk * W
                 for part in range(2):
                     copies.append(
                         pltpu.make_async_copy(
                             incident.at[part, :, at : at + W],
-                            out.at[16 * part : 16 * part + 16, i * W : i * W + W],
+                            outs[2 * chunk + side].at[16 * part : 16 * part + 16, i * W : i * W + W],
                             sems.at[chunk, side, i, part],
                         )
                     )
@@ -92,10 +92,9 @@
 
 
 def pack(incident, phase):
-    rows = incident.shape[2] // COLS
     widths = [BELOW * W + TILES * 128, ABOVE * W + TILES * 128] * CHUNKS
     return pl.pallas_call(
-        functools.partial(pack_kernel, rows),
+        pack_kernel,
         out_shape=tuple(jax.ShapeDtypeStruct((32, w), jnp.float32) for w in widths),
         in_specs=[pl.BlockSpec(memory_space=pl.ANY)] * 2,
         out_specs=(pl.BlockSpec(memory_space=pltpu.VMEM),) * len(widths),
@@ -115,9 +114,8 @@
     "border": ((-8, 8), (47, 10)),
     "whole": ((-7, 64),),
 }
-OWN_ROWS = {"inner": ((0, 64),), "border": ((0, 16), (47, 64)), "whole": ((0, 64),)}
-OWN_PHASES = {"inner": ((0, 64),), "border": ((0, 16), (40, 64)), "whole": ((0, 64),)}
-TABLE_ROWS = {"inner": ((1, 9),), "border": ((0, 3), (6, 11)), "whole": ((0, 11),)}
+OWN_PHASES = {"inner": ((0, 64),), "border": ((0, 8), (48, 64)), "whole": ((0, 64),)}
+TABLE_ROWS = {"inner": ((1, 9),), "border": ((0, 2), (8, 11)), "whole": ((0, 11),)}
 
 
 def advance_gauge(gauge_in, gauge):
@@ -140,20 +138,31 @@
     lax.fori_loop(0, 10, advance, tuple(strands))
 
 
-def sweep_kernel(mode, chunk, incident, phase, gauge_in, *refs):
-    below = above = inner_inten = stage = None
-    if mode != "inner":
-        below, above, refs = refs[0], refs[1], refs[2:]
+def sweep_kernel(mode, chunk, phase, *refs):
+    below = above = stage = state_out = None
+    departures = []
     if mode == "border":
-        inner_inten, refs = refs[0], refs[1:]
-    raw_out, inten_out, last_out, own, wave, phases, tab, last, gauge, raw, stage, sems = refs
-    arrivals = [
-        pltpu.make_async_copy(incident.at[:, :, lo * COLS : hi * COLS], own.at[:, :, lo * COLS : hi * COLS], sems.at[k])
-        for k, (lo, hi) in enumerate(OWN_ROWS[mode])
-    ]
-    for c in arrivals:
-        c.start()
-    advance_gauge(gauge_in, gauge)
+        below, above, inner_raw, inner_inten, state_in = refs[:5]
+        inner_raw_out, raw_out, inten_out, last_out, tab, wave, gauge, phases, last, raw, stage, sems = refs[8:]
+        departures = [
+            pltpu.make_async_copy(inner_inten.at[2:13], inten_out.at[2:13], sems.at[0]),
+            pltpu.make_async_copy(inner_raw, inner_raw_out, sems.at[1]),
+        ]
+        for c in departures:
+            c.start()
+    elif mode == "inner":
+        incident, gauge_in, raw, inten_out, last_out, tab, wave, gauge, state_out, own, phases, last, sems = refs
+    else:
+        incident, gauge_in, below, above, raw_out, inten_out, last_out, tab, wave, gauge, own, phases, last, raw, sems = refs
+    if mode != "border":
+        half = incident.shape[2] // 2
+        arrivals = [
+            pltpu.make_async_copy(incident.at[:, :, k * half : k * half + half], own.at[:, :, k * half : k * half + half], sems.at[k])
+            for k in range(2)
+        ]
+        for c in arrivals:
+            c.start()
+        advance_gauge(gauge_in, gauge)
 
     for t in range(TILES):
         for lo, hi in OWN_PHASES[mode]:
@@ -194,21 +203,44 @@
         return tuple(rolled)
 
     for lo, hi in TABLE_ROWS[mode]:
-        lax.fori_loop(lo, hi, tables, (jnp.zeros((8, 128), jnp.float32),) * (6 * TILES))
-    departures = [pltpu.make_async_copy(last, last_out, sems.at[2])]
-    departures[0].start()
-
-    def regauge(row, at, re_of, im_of):
+        start = []
+        for t in range(TILES):
+            for b in range(3):
+                if mode == "border" and lo > 0:
+                    start += [pltpu.roll(x, 1, 0) for x in turn(phases[b, t, 8 * lo - 8 : 8 * lo, :])]
+                else:
+                    start += [jnp.zeros((8, 128), jnp.float32)] * 2
+        lax.fori_loop(lo, hi, tables, tuple(start))
+    departures.append(pltpu.make_async_copy(last, last_out, sems.at[2]))
+    departures[-1].start()
+
+    def regauge(row, re_of, im_of):
         er, ei = gauge[row + 10, 0], gauge[row + 10, 1]
         for t in range(TILES):
             tr, ti = times(re_of(t), im_of(t), er, ei)
-            wave[at, 0, :, t * 128 : t * 128 + 128] = tr
-            wave[at, 1, :, t * 128 : t * 128 + 128] = ti
+            wave[row + 8, 0, :, t * 128 : t * 128 + 128] = tr
+            wave[row + 8, 1, :, t * 128 : t * 128 + 128] = ti
+
+    if mode != "inner":
+        for ref, count, first in ((below, BELOW, -BELOW), (above, ABOVE, 64)):
+            for i in range(count):
+                lanes = lambda t, i=i: slice(i * W + t * 128, i * W + t * 128 + 128)
+                regauge(first + i, lambda t, ref=ref: ref[0:16, lanes(t)], lambda t, ref=ref: ref[16:32, lanes(t)])
+    if mode != "border":
+        for c in arrivals:
+            c.wait()
+
+        @pl.loop(0, 16)
+        def _(j):
+            for k in range(4):
+                row = 4 * j + k
+                lanes = lambda t, row=row: pl.ds(pl.multiple_of(row * COLS + chunk * W + t * 128, 128), 128)
+                regauge(row, lambda t: own[0, :, lanes(t)], lambda t: own[1, :, lanes(t)])
 
     def packet(r0, low, place, tile, state, steps):
         lanes = pl.ds(pl.multiple_of(tile * 128, 128), 128)
-        tr = wave[r0 - low, 0, :, lanes]
-        ti = wave[r0 - low, 1, :, lanes]
+        tr = wave[r0 + 8, 0, :, lanes]
+        ti = wave[r0 + 8, 1, :, lanes]
         after = []
         for n in range(steps):
             if n == 0:
@@ -227,53 +259,33 @@
             raw[tile, place + r0 - low, 0] = nr
             raw[tile, place + r0 - low, 1] = ni
             inten = SCALE * SCALE * (nr * nr + ni * ni)
-            if mode == "inner":
-                inten_out[r0 - low, :, lanes] = inten
-            elif mode == "border":
-                stage[place + r0 - low, :, lanes] = inten
+            row = r0 + 7
+            off = pl.multiple_of((row % 4) * W + tile * 128, 128)
+            if mode != "border":
+                inten_out[row // 4, :, pl.ds(off, 128)] = inten
+            elif low < 0:
+                stage[(row + 24) // 4 % 6, :, pl.ds(off, 128)] = inten
             else:
-                row = r0 + 7
-                off = pl.multiple_of((row % 4) * W + tile * 128, 128)
-                inten_out[row // 4, :, pl.ds(off, 128)] = inten
+                stage[row // 4 - 11, :, pl.ds(off, 128)] = inten
         return tuple(after)
 
-    for c in arrivals:
-        c.wait()
     place = 0
     for low, count in PARTS[mode]:
         high = low + count + 15
-        if low < 0:
-            for i in range(BELOW):
-                lanes = lambda t, i=i: slice(i * W + t * 128, i * W + t * 128 + 128)
-                regauge(i - BELOW, i - BELOW - low, lambda t: below[0:16, lanes(t)], lambda t: below[16:32, lanes(t)])
-        if high > 64:
-            for i in range(ABOVE):
-                lanes = lambda t, i=i: slice(i * W + t * 128, i * W + t * 128 + 128)
-                regauge(64 + i, 64 + i - low, lambda t: above[0:16, lanes(t)], lambda t: above[16:32, lanes(t)])
-
-        def own_row(row, low=low):
-            lanes = lambda t: pl.ds(pl.multiple_of(row * COLS + chunk * W + t * 128, 128), 128)
-            regauge(row, row - low, lambda t: own[0, :, lanes(t)], lambda t: own[1, :, lanes(t)])
-
-        first, end = max(low, 0), min(high, 63) + 1
-        fours = (end - first) // 4
-
-        @pl.loop(0, fours)
-        def _(j, first=first, own_row=own_row):
-            for k in range(4):
-                own_row(first + 4 * j + k)
-
-        for row in range(first + 4 * fours, end):
-            own_row(row)
 
         @pl.loop(0, TILES)
         def _(tile, low=low, high=high, count=count, place=place):
             @pl.loop(0, 2)
             def _(odd):
                 top = high - odd
-                state = ()
-                for i in range(8):
-                    state = packet(top - 2 * i, low, place, tile, state, i + 1)
+                if mode == "border" and low < 0:
+                    state = tuple(state_in[2 * tile + odd, k] for k in range(16))
+                    first = packet(0, low, place, tile, (), 1)
+                    state = tuple(jnp.where(odd == 1, f, x) for f, x in zip(first, state[:2])) + state[2:]
+                else:
+                    state = ()
+                    for i in range(8):
+                        state = packet(top - 2 * i, low, place, tile, state, i + 1)
                 group = 5 if count == 10 else 4
 
                 def several(j, state):
@@ -281,61 +293,77 @@
                         state = packet(top - 16 - 2 * group * j - 2 * i, low, place, tile, state, 9)
                     return state
 
-                lax.fori_loop(0, count // 2 // group, several, state)
-
-            if mode != "border":
+                state = lax.fori_loop(0, count // 2 // group, several, state)
+                if mode == "inner":
+                    for k in range(16):
+                        state_out[2 * tile + odd, k] = state[k]
+
+            if mode == "whole":
                 pltpu.make_async_copy(raw.at[tile], raw_out.at[tile], sems.at[3 + tile]).start()
 
         place += count
     if mode == "border":
+        stage[1, :, 3 * W : 4 * W] = inner_inten[1, :, 3 * W : 4 * W]
+        stage[2, :, 0 : 3 * W] = inner_inten[13, :, 0 : 3 * W]
+        departures += [
+            pltpu.make_async_copy(stage.at[0:2], inten_out.at[0:2], sems.at[5]),
+            pltpu.make_async_copy(stage.at[2:5], inten_out.at[13:16], sems.at[6]),
+            pltpu.make_async_copy(raw, raw_out, sems.at[3]),
+        ]
+        for c in departures[-3:]:
+            c.start()
+    for c in departures:
+        c.wait()
+    if mode == "whole":
         for tile in range(TILES):
-            pltpu.make_async_copy(raw.at[tile], raw_out.at[tile], sems.at[3 + tile]).start()
-        for row in range(64):
-            if row < 7:
-                value = stage[row + 1]
-            elif row < 55:
-                value = inner_inten[row - 7]
-            else:
-                value = stage[row - 46]
-            inten_out[row // 4, :, (row % 4) * W : (row % 4) * W + W] = value
-    departures[0].wait()
-    for tile in range(TILES):
-        pltpu.make_async_copy(raw.at[tile], raw_out.at[tile], sems.at[3 + tile]).wait()
+            pltpu.make_async_copy(raw.at[tile], raw_out.at[tile], sems.at[3 + tile]).wait()
 
 
 def whole_block(shape):
     return pl.BlockSpec(shape, lambda i: (0,) * len(shape))
 
 
-def sweep(mode, incident, phase, gauge, chunk, *more):
+def sweep(mode, chunk, incident, phase, gauge, *more):
     total = sum(count for _, count in PARTS[mode])
-    tall = max(count for _, count in PARTS[mode]) + 16
-    shapes = ((TILES, total, 2, 16, 128), (48, 16, W) if mode == "inner" else (16, 16, 4 * W), (2, TILES, 88, 128))
+    shapes = ((TILES, total, 2, 16, 128), (16, 16, 4 * W), (2, TILES, 88, 128))
+    kept = ((5, 2, TILES, 88, 128), (81, 2, 16, W), (88, 2, 16, 128))
+    f32 = lambda shape: jax.ShapeDtypeStruct(shape, jnp.float32)
     vmem, hbm = pl.BlockSpec(memory_space=pltpu.VMEM), pl.BlockSpec(memory_space=pltpu.HBM)
+    outs = [pltpu.HBM(shapes[0], jnp.float32), f32(shapes[1]), pltpu.HBM(shapes[2], jnp.float32)]
+    out_specs = [hbm, vmem, hbm]
+    scratch = [pltpu.VMEM((3, TILES, 88, 128), jnp.float32), pltpu.VMEM(shapes[2], jnp.float32)]
+    aliases = {}
+    if mode == "border":
+        ops = [phase, *more]
+        in_specs = [vmem] * len(ops)
+        aliases = {len(ops) - 3 + k: 4 + k for k in range(3)}
+        outs = [pltpu.HBM(more[2].shape, jnp.float32), outs[0], pltpu.HBM(shapes[1], jnp.float32), outs[2]]
+        out_specs = [hbm] * 4
+        scratch += [pltpu.VMEM(shapes[0], jnp.float32), pltpu.VMEM((6, 16, 4 * W), jnp.float32)]
+    else:
+        ops = [phase, in_hbm(incident), gauge, *more]
+        in_specs = [vmem, pl.BlockSpec(memory_space=pl.ANY)] + [vmem] * (1 + len(more))
+        scratch.insert(0, pltpu.VMEM(incident.shape, jnp.float32))
+    if mode == "whole":
+        scratch = [pltpu.VMEM(x, jnp.float32) for x in kept] + scratch + [pltpu.VMEM(shapes[0], jnp.float32)]
+    else:
+        outs += [f32(x) for x in kept]
+        out_specs += [vmem] * 3
+    if mode == "inner":
+        outs[0], out_specs[0] = f32(shapes[0]), vmem
+        outs.append(f32((2 * TILES, 16, 16, 128)))
+        out_specs.append(vmem)
     return pl.pallas_call(
         functools.partial(sweep_kernel, mode, chunk),
-        out_shape=(
-            pltpu.HBM(shapes[0], jnp.float32),
-            jax.ShapeDtypeStruct(shapes[1], jnp.float32),
-            pltpu.HBM(shapes[2], jnp.float32),
-        ),
-        in_specs=[pl.BlockSpec(memory_space=pl.ANY)] + [vmem] * (2 + len(more)),
-        out_specs=(hbm, vmem, hbm),
-        scratch_shapes=[
-            pltpu.VMEM(incident.shape, jnp.float32),
-            pltpu.VMEM((tall, 2, 16, W), jnp.float32),
-            pltpu.VMEM((3, TILES, 88, 128), jnp.float32),
-            pltpu.VMEM((5, 2, TILES, 88, 128), jnp.float32),
-            pltpu.VMEM((2, TILES, 88, 128), jnp.float32),
-            pltpu.VMEM((88, 2, 16, 128), jnp.float32),
-            pltpu.VMEM((TILES, total, 2, 16, 128), jnp.float32),
-            pltpu.VMEM((18, 16, W), jnp.float32),
-            pltpu.SemaphoreType.DMA((3 + TILES,)),
-        ],
+        out_shape=tuple(outs),
+        in_specs=in_specs,
+        out_specs=tuple(out_specs),
+        scratch_shapes=scratch + [pltpu.SemaphoreType.DMA((7,))],
+        input_output_aliases=aliases,
         compiler_params=pltpu.CompilerParams(vmem_limit_bytes=24 * 1024 * 1024),
         cost_estimate=pl.CostEstimate(flops=total * 16 * W * 120, bytes_accessed=8 * 1024 * 1024, transcendentals=0),
         name="sweep",
-    )(in_hbm(incident), phase, gauge, *more)
+    )(*ops)
 
 
 def merge_kernel(gauge_in, inner, border, whole, last_inner, last_border, last_whole, out, gauge):
@@ -430,8 +458,9 @@
     edges = pack(incident, phase_table)
     below, above = [], []
     for chunk in range(CHUNKS):
-        below.append(passed_along(edges[2 * chunk], "lat", 1))
-        above.append(passed_along(edges[2 * chunk + 1], "lat", -1))
+        lower, upper = edges[2 * chunk], edges[2 * chunk + 1]
+        below.append(passed_along(lower, "lat", 1))
+        above.append(passed_along(upper, "lat", -1))
     angle = -0.5 * detuning[None, :] * jnp.array([-10.0, -9.0, -8.0, -7.0, -6.0, -5.0, -4.0, -3.0, 8.0], jnp.float32)[:, None]
     gauge = jnp.stack([jnp.cos(angle), jnp.sin(angle)], axis=1)
     gauge = jnp.broadcast_to(gauge[..., None], gauge.shape + (128,))
@@ -443,10 +472,12 @@
         for c in range(CHUNKS)
     ]
 
-    raw_inner, inten_inner, last_inner = sweep("inner", incident, phase_table, gauge, 0)
-    raw_border, inten0, last_border = sweep("border", incident, phase_table, gauge, 0, below[0], above[0], inten_inner)
+    raw_inner, inten_inner, last_inner, *kept, state = sweep("inner", 0, incident, phase_table, gauge)
+    raw_inner, raw_border, inten0, last_border = sweep(
+        "border", 0, None, phase_table, None, below[0], above[0], raw_inner, inten_inner, state, *kept
+    )[:4]
     there0 = exchange(inten0)
-    raw_whole, inten1, last_whole = sweep("whole", incident, phase_table, gauge, 1, below[1], above[1])
+    raw_whole, inten1, last_whole = sweep("whole", 1, incident, phase_table, gauge, below[1], above[1])
     there1 = exchange(inten1)
     estimate0 = deconvolve(there0.reshape(256, 4 * W), response, scaled, measured[0])
     back0 = exchange(estimate0.reshape(16, 16, 4 * W))

time: 131 us -> 128 us (0.977)
  Pallas kernels: 32.2 us -> 28.6 us
  matrix products: 19.5 us -> 21 us
    pallas_call x4, Pallas kernels: 23.4 us -> 19.9 us  [the longest x3 17.7 us: sweep(): pl.pallas_call(functools.partial(sweep_kernel, mode, chunk), out_shape=tu...]
  transfers between devices with their start and end apart: 8 -> 8, of which waited for: 6 -> 6; matrix products, arithmetic and copies ran while one was open for 13% -> 14% of each run, Pallas kernels for 18% -> 17%
where the time goes in v1:
time: 128 us
  waiting for transfers between devices  43.6 us (34%)
  starting transfers between devices  30.4 us (24%)
  Pallas kernels  28.6 us (22%)
  matrix products  21 us (16%)
  local copies, waits for them, and re-layouts  2.65 us (2%)
    all_to_all x4, waiting for transfers between devices, exchange(): return lax.all_to_all(x, 'ang', split_axis=0, concat_axis=0, tiled=True)  26.6 us
    all_to_all x4, starting transfers between devices, exchange(): return lax.all_to_all(x, 'ang', split_axis=0, concat_axis=0, tiled=True)  19 us
    pallas_call x3, Pallas kernels, sweep(): pl.pallas_call(functools.partial(sweep_kernel, mode, chunk), out_shape=tu...  17.7 us
    ppermute x4, waiting for transfers between devices, passed_along(): lax.ppermute(x, axis, [(i, (i + by) % devices) for i in range(devices)])  17 us
    ppermute x4, starting transfers between devices, passed_along(): lax.ppermute(x, axis, [(i, (i + by) % devices) for i in range(devices)])  11.4 us
    dot_general x12, matrix products, deconvolve(): lax.dot_general(scaled, measured / blurred, (((0,), (0,)), ((), ())), pre...  11.3 us
    dot_general x12, matrix products, deconvolve(): jnp.dot(response, estimate, precision=lax.Precision.HIGH, preferred_eleme...  9.75 us
    pallas_call x1, Pallas kernels, merge(): pl.pallas_call(merge_kernel, grid=(1,), out_shape=jax.ShapeDtypeStruct((2...  5.73 us
  transfers between devices with their start and end apart: 8, of which 6 were waited for; matrix products, arithmetic and copies ran while one was open for 14% of the time, Pallas kernels for 17%

profile of v1, /device:TPU:24, one launch (start us, length us, event | category | flops | bytes accessed | tf_op | source)
XLA Modules:
  0.0 127.7 jit_solution(4219484550433539062)
XLA Ops:
  0.6 0.0 copy-start.6
  0.6 0.0 copy-start
  0.7 0.0 copy-start.7
  0.7 2.2 %pack.1 = (f32[32,2048]{1,0:T(8,128)S(1)}, f32[32,2560]{1,0:T(8,128)S(1)}, f32[32,2048]{1,0:T(8,128)S(1)}, f32[32,2560]{1,0:T(8,128)S(1)}) custom-call(f32[2,16,32768]{2,1,0:T(8,128)} %refs_0_.3, s32[3,32768]{1,0:T(4,128)} %phase.7), custom_call_target="tpu_custom_call" | custom-call | bytes 2097152 | tf_op jit(solution)/shard_map/pack/pallas_call | solution.py:96
  2.8 0.8 collective-permute-start.1
  3.7 4.9 %collective-permute-start = (f32[32,2048]{1,0:T(8,128)S(1)}, f32[32,2048]{1,0:T(8,128)S(1)}, u32[]{:S(2)}, u32[]{:S(2)}) collective-permute-start(f32[32,2048]{1,0:T(8,128)S(1)} %get-tuple-element.21), channel_id=1, source_target_pairs={{0,16},{16,32},{32,48},{48,64},{64,80},{80,96},{96,112},{112,0},{1... | collective-permute-start | bytes 786440 | tf_op jit(solution)/shard_map/ppermute | solution.py:28
  8.6 0.0 copy-done.7
  8.6 0.0 copy-done.6
  8.6 0.2 multiply_cosine_fusion
  8.8 0.1 broadcast_in_dim.2.refs_1_.gauge_in
  8.9 0.0 copy-done
  8.9 0.0 copy-start.1
  8.9 6.1 %sweep.3 = (f32[2,48,2,16,128]{4,3,2,1,0:T(8,128)S(1)}, f32[16,16,1024]{2,1,0:T(8,128)S(1)}, f32[2,2,88,128]{3,2,1,0:T(8,128)}, f32[5,2,2,88,128]{4,3,2,1,0:T(8,...) custom-call(s32[3,32768]{1,0:T(4,128)S(1)} %copy-done, ...), custom_call_target="tpu_custom_call" | custom-call | flops 23592960 | bytes 8388608 | tf_op jit(solution)/shard_map/sweep/pallas_call | solution.py:356
  15.0 0.0 collective-permute-done.refs_0_
  15.0 1.0 collective-permute-done.1.refs_1_
  16.0 2.7 %sweep.4 = (f32[2,48,2,16,128]{4,3,2,1,0:T(8,128)}, f32[2,18,2,16,128]{4,3,2,1,0:T(8,128)}, f32[16,16,1024]{2,1,0:T(8,128)}, f32[2,2,88,128]{3,2,1,0:T(8,128)}, ...) custom-call(s32[3,32768]{1,0:T(4,128)S(1)} %copy-done, ...), custom_call_target="tpu_custom_call", output_to_operand_aliasing={{4}: (6, {}), {5}: (7, {}), {6}: (8, {})} | custom-call | flops 8847360 | bytes 8388608 | tf_op jit(solution)/shard_map/sweep/pallas_call | solution.py:356
  18.7 0.0 copy-start.2
  18.7 6.5 %all-to-all-start.1 = ((f32[16,16,1024]{2,1,0:T(8,128)}), f32[16,16,1024]{2,1,0:T(8,128)}, u32[]{:S(2)}, u32[]{:S(2)}) async-start(f32[16,16,1024]{2,1,0:T(8,128)} %get-tuple-element.38), calls=%async_computation.1 | async-start | bytes 2097152 | tf_op jit(solution)/shard_map/all_to_all | solution.py:453
  25.3 0.1 collective-permute-start.3
  25.4 5.6 %collective-permute-start.2 = (f32[32,2048]{1,0:T(8,128)S(1)}, f32[32,2048]{1,0:T(8,128)S(1)}, u32[]{:S(2)}, u32[]{:S(2)}) collective-permute-start(f32[32,2048]{1,0:T(8,128)S(1)} %get-tuple-element.31), channel_id=1, source_target_pairs={{0,16},{16,32},{32,48},{48,64},{64,80},{80,96},{96,112},{112,0},{1... | collective-permute-start | bytes 786440 | tf_op jit(solution)/shard_map/ppermute | solution.py:28
  31.0 0.0 copy-done.2
  31.0 2.5 %fusion.24 = (s32[256,256]{1,0:T(8,128)S(1)}, s32[256,256]{1,0:T(8,128)S(1)}, s32[256,256]{1,0:T(8,128)S(1)}, s32[256,256]{1,0:T(8,128)}, s32[256,256]{1,0:T(8,1...) fusion(s32[256,2048]{1,0:T(8,128)} %param.10), kind=kLoop, calls=%fused_computation.55 | loop fusion | bytes 4194304 | tf_op jit(solution)/shard_map/slice | solution.py:471
  33.6 9.6 %collective-permute-done.2.refs_2_ = f32[32,2048]{1,0:T(8,128)S(1)} collective-permute-done((f32[32,2048]{1,0:T(8,128)S(1)}, f32[32,2048]{1,0:T(8,128)S(1)}, u32[]{:S(2)}, u32[]{:S(2)}) %collective-permute-start.2) | collective-permute-done | bytes 262176 | tf_op jit(solution)/shard_map/ppermute | solution.py:28
  43.2 6.4 %collective-permute-done.3.refs_3_ = f32[32,2560]{1,0:T(8,128)S(1)} collective-permute-done((f32[32,2560]{1,0:T(8,128)S(1)}, f32[32,2560]{1,0:T(8,128)S(1)}, u32[]{:S(2)}, u32[]{:S(2)}) %collective-permute-start.3) | collective-permute-done | bytes 327712 | tf_op jit(solution)/shard_map/ppermute | solution.py:28
  49.6 0.0 copy-done.1
  49.6 8.9 %sweep.5 = (f32[2,64,2,16,128]{4,3,2,1,0:T(8,128)}, f32[16,16,1024]{2,1,0:T(8,128)}, f32[2,2,88,128]{3,2,1,0:T(8,128)}) custom-call(s32[3,32768]{1,0:T(4,128)S(1)} %copy-done, f32[2,16,32768]{2,1,0:T(8,128)} %refs_0_.3, f32[9,2,16,128]{3,2,1,0:T(8,128)S(1)} %broadcast_in_dim.2.refs_1_.gauge_in, f32[32,2048]{1,0:T(8,128)S(1)} %collective-permute-done.2.refs_2_, ...), custom_call_target="tpu_custom_call" | custom-call | flops 31457280 | bytes 8388608 | tf_op jit(solution)/shard_map/sweep/pallas_call | solution.py:356
  58.5 0.0 copy-start.3
  58.5 0.0 copy-start.4
  58.5 0.0 all-to-all-done.1
  58.5 5.1 %all-to-all-start = ((f32[16,16,1024]{2,1,0:T(8,128)}), f32[16,16,1024]{2,1,0:T(8,128)S(1)}, u32[]{:S(2)}, u32[]{:S(2)}) async-start(f32[16,16,1024]{2,1,0:T(8,128)} %get-tuple-element.37), calls=%async_computation | async-start | bytes 2097152 | tf_op jit(solution)/shard_map/all_to_all | solution.py:453
  63.6 0.0 copy-done.3
  63.6 2.0 %fusion.23 = f32[256,1024]{1,0:T(8,128)S(1)} fusion(f32[256,1024]{1,0:T(8,128)} %bitcast, f32[256,256]{1,0:T(8,128)S(1)} %copy-done.2, s32[256,256]{1,0:T(8,128)S(1)} %get-tuple-element.42, s32[256,256]{1,0:T(8,128)S(1)} %copy-done.3, s32[256,256]{1,0:T(8,128)S(1)} %copy-done.4, s32[256,256]{1,0:T(8,128)} %get-tuple-element.45), kind=kOutput, calls=%fused_computation.47 | convolution fusion | flops 404226048 | bytes 3407872 | tf_op jit(solution)/shard_map/dot_general | solution.py:440
  65.6 0.0 copy-start.5
  65.6 1.9 %convolution_multiply_fusion.11 = f32[256,1024]{1,0:T(8,128)S(1)} fusion(f32[256,1024]{1,0:T(8,128)} %bitcast, f32[256,1024]{1,0:T(8,128)S(1)} %fusion.23, f32[256,256]{1,0:T(8,128)S(1)} %copy-done.2, f32[256]{0:T(256)S(1)} %reduce_sum.9), kind=kOutput, calls=%fused_computation.44 | convolution fusion | flops 402980864 | bytes 3408896 | tf_op jit(solution)/shard_map/dot_general | solution.py:441
  67.5 0.7 fusion.21
  68.3 0.7 convolution_multiply_fusion.10
  68.9 0.7 fusion.19
  69.6 0.7 convolution_multiply_fusion.9
  70.3 0.7 fusion.17
  71.0 0.7 convolution_multiply_fusion.8
  71.7 0.7 fusion.15
  72.4 0.7 convolution_multiply_fusion.7
  73.0 0.7 fusion.13
  73.8 1.6 %convolution_multiply_fusion.6 = f32[256,1024]{1,0:T(8,128)} fusion(f32[256,1024]{1,0:T(8,128)S(1)} %convolution_multiply_fusion.7, f32[256,1024]{1,0:T(8,128)S(1)} %fusion.13, f32[256,256]{1,0:T(8,128)S(1)} %copy-done.2, f32[256]{0:T(256)S(1)} %reduce_sum.9), kind=kOutput, calls=%fused_computation.24 | convolution fusion | flops 402980864 | bytes 3408896 | tf_op jit(solution)/shard_map/dot_general | solution.py:441
  75.4 4.6 %all-to-all-done = f32[16,16,1024]{2,1,0:T(8,128)S(1)} async-done(((f32[16,16,1024]{2,1,0:T(8,128)}), f32[16,16,1024]{2,1,0:T(8,128)S(1)}, u32[]{:S(2)}, u32[]{:S(2)}) %all-to-all-start) | async-done | bytes 1048608 | tf_op jit(solution)/shard_map/all_to_all | solution.py:453
  80.0 0.7 fusion.11
  80.7 0.7 convolution_multiply_fusion.5
  81.3 0.7 fusion.9
  82.0 0.7 convolution_multiply_fusion.4
  82.7 0.7 fusion.7
  83.4 0.9 convolution_multiply_fusion.3
  84.3 0.7 fusion.5
  85.0 0.7 convolution_multiply_fusion.2
  85.7 3.7 %all-to-all-start.3 = ((f32[16,16,1024]{2,1,0:T(8,128)}), f32[16,16,1024]{2,1,0:T(8,128)S(1)}, u32[]{:S(2)}, u32[]{:S(2)}) async-start(f32[16,16,1024]{2,1,0:T(8,128)} %bitcast.15), calls=%async_computation.3 | async-start | bytes 2097152 | tf_op jit(solution)/shard_map/all_to_all | solution.py:453
  89.3 0.7 fusion.3
  90.1 0.7 convolution_multiply_fusion.1
  90.7 0.7 fusion.1
  91.4 1.6 %convolution_multiply_fusion = f32[256,1024]{1,0:T(8,128)} fusion(f32[256,1024]{1,0:T(8,128)S(1)} %convolution_multiply_fusion.1, f32[256,1024]{1,0:T(8,128)S(1)} %fusion.1, f32[256,256]{1,0:T(8,128)S(1)} %copy-done.2, f32[256]{0:T(256)S(1)} %reduce_sum.9), kind=kOutput, calls=%fused_computation | convolution fusion | flops 402980864 | bytes 3408896 | tf_op jit(solution)/shard_map/dot_general | solution.py:441
  93.1 12.8 %all-to-all-done.3.block = f32[16,16,1024]{2,1,0:T(8,128)S(1)} async-done(((f32[16,16,1024]{2,1,0:T(8,128)}), f32[16,16,1024]{2,1,0:T(8,128)S(1)}, u32[]{:S(2)}, u32[]{:S(2)}) %all-to-all-start.3) | async-done | bytes 1048608 | tf_op jit(solution)/shard_map/all_to_all | solution.py:453
  105.9 3.7 %all-to-all-start.2 = ((f32[16,16,1024]{2,1,0:T(8,128)}), f32[16,16,1024]{2,1,0:T(8,128)S(1)}, u32[]{:S(2)}, u32[]{:S(2)}) async-start(f32[16,16,1024]{2,1,0:T(8,128)} %bitcast.14), calls=%async_computation.2 | async-start | bytes 2097152 | tf_op jit(solution)/shard_map/all_to_all | solution.py:453
  109.5 5.7 %merge.1 = f32[2,16,32768]{2,1,0:T(8,128)} custom-call(f32[9,2,16,128]{3,2,1,0:T(8,128)} %copy-done.1, f32[2,48,2,16,128]{4,3,2,1,0:T(8,128)} %get-tuple-element.29.inner, f32[2,18,2,16,128]{4,3,2,1,0:T(8,128)} %get-tuple-element.30.border, f32[2,64,2,16,128]{4,3,2,1,0:T(8,128)} %get-tuple-element.33.whole, f32[2,2,88,128]{3,2,1,0:T(8,128)} %get-tuple-element.34.last_inner, ...), custom_call_target="tpu_custom_call" | custom-call | bytes 8388608 | tf_op jit(solution)/shard_map/merge/pallas_call | solution.py:398
  115.2 1.5 %place.2.refs_0_ = f32[16,32768]{1,0:T(8,128)} custom-call(f32[16,16,1024]{2,1,0:T(8,128)S(1)} %all-to-all-done.3.block), custom_call_target="tpu_custom_call" | custom-call | bytes 4194304 | tf_op jit(solution)/shard_map/place/pallas_call | solution.py:425
  116.8 9.3 %all-to-all-done.2.block = f32[16,16,1024]{2,1,0:T(8,128)S(1)} async-done(((f32[16,16,1024]{2,1,0:T(8,128)}), f32[16,16,1024]{2,1,0:T(8,128)S(1)}, u32[]{:S(2)}, u32[]{:S(2)}) %all-to-all-start.2) | async-done | bytes 1048608 | tf_op jit(solution)/shard_map/all_to_all | solution.py:453
  126.0 1.5 %place.3 = f32[16,32768]{1,0:T(8,128)} custom-call(f32[16,16,1024]{2,1,0:T(8,128)S(1)} %all-to-all-done.2.block, f32[16,32768]{1,0:T(8,128)} %place.2.refs_0_), custom_call_target="tpu_custom_call", output_to_operand_aliasing={{}: (1, {})} | custom-call | bytes 4194304 | tf_op jit(solution)/shard_map/place/pallas_call | solution.py:425
  (5 shorter events, 0.1 us)
Async XLA Ops:
  0.6 7.9 %copy-start.6 = (f32[9]{0:T(128)S(1)}, f32[9]{0:T(128)}, u32[]{:S(2)}) copy-start(f32[9]{0:T(128)} %constant.8.clone) | copy-start | bytes 112
  0.6 8.3 %copy-start = (s32[3,32768]{1,0:T(4,128)S(1)}, s32[3,32768]{1,0:T(4,128)}, u32[]{:S(2)}) copy-start(s32[3,32768]{1,0:T(4,128)} %phase.7) | copy-start | bytes 1179652
  0.7 7.9 %copy-start.7 = (f32[16]{0:T(128)S(1)}, f32[16]{0:T(128)}, u32[]{:S(2)}) copy-start(f32[16]{0:T(128)} %param.7) | copy-start | bytes 196
  2.8 13.1 %collective-permute-start.1 = (f32[32,2560]{1,0:T(8,128)S(1)}, f32[32,2560]{1,0:T(8,128)S(1)}, u32[]{:S(2)}, u32[]{:S(2)}) collective-permute-start(f32[32,2560]{1,0:T(8,128)S(1)} %get-tuple-element.22), channel_id=1, source_target_pairs={{0,112},{16,0},{32,16},{48,32},{64,48},{80,64},{96,80},{112,96},{1... | collective-permute-start | bytes 983048 | tf_op jit(solution)/shard_map/ppermute | solution.py:28
  3.7 11.4 %collective-permute-start = (f32[32,2048]{1,0:T(8,128)S(1)}, f32[32,2048]{1,0:T(8,128)S(1)}, u32[]{:S(2)}, u32[]{:S(2)}) collective-permute-start(f32[32,2048]{1,0:T(8,128)S(1)} %get-tuple-element.21), channel_id=1, source_target_pairs={{0,16},{16,32},{32,48},{48,64},{64,80},{80,96},{96,112},{112,0},{1... | collective-permute-start | bytes 786440 | tf_op jit(solution)/shard_map/ppermute | solution.py:28
  8.9 40.7 %copy-start.1 = (f32[9,2,16,128]{3,2,1,0:T(8,128)}, f32[9,2,16,128]{3,2,1,0:T(8,128)S(1)}, u32[]{:S(2)}) copy-start(f32[9,2,16,128]{3,2,1,0:T(8,128)S(1)} %broadcast_in_dim.2.refs_1_.gauge_in) | copy-start | bytes 442372
  18.7 12.3 %copy-start.2 = (f32[256,256]{1,0:T(8,128)S(1)}, f32[256,256]{1,0:T(8,128)}, u32[]{:S(2)}) copy-start(f32[256,256]{1,0:T(8,128)} %param.9) | copy-start | bytes 786436
  18.7 39.8 %all-to-all-start.1 = ((f32[16,16,1024]{2,1,0:T(8,128)}), f32[16,16,1024]{2,1,0:T(8,128)}, u32[]{:S(2)}, u32[]{:S(2)}) async-start(f32[16,16,1024]{2,1,0:T(8,128)} %get-tuple-element.38), calls=%async_computation.1 | async-start | bytes 2097152 | tf_op jit(solution)/shard_map/all_to_all | solution.py:453
  25.3 24.3 %collective-permute-start.3 = (f32[32,2560]{1,0:T(8,128)S(1)}, f32[32,2560]{1,0:T(8,128)S(1)}, u32[]{:S(2)}, u32[]{:S(2)}) collective-permute-start(f32[32,2560]{1,0:T(8,128)S(1)} %get-tuple-element.32), channel_id=1, source_target_pairs={{0,112},{16,0},{32,16},{48,32},{64,48},{80,64},{96,80},{112,96},{1... | collective-permute-start | bytes 983048 | tf_op jit(solution)/shard_map/ppermute | solution.py:28
  25.4 17.8 %collective-permute-start.2 = (f32[32,2048]{1,0:T(8,128)S(1)}, f32[32,2048]{1,0:T(8,128)S(1)}, u32[]{:S(2)}, u32[]{:S(2)}) collective-permute-start(f32[32,2048]{1,0:T(8,128)S(1)} %get-tuple-element.31), channel_id=1, source_target_pairs={{0,16},{16,32},{32,48},{48,64},{64,80},{80,96},{96,112},{112,0},{1... | collective-permute-start | bytes 786440 | tf_op jit(solution)/shard_map/ppermute | solution.py:28
  58.5 5.1 %copy-start.3 = (s32[256,256]{1,0:T(8,128)S(1)}, s32[256,256]{1,0:T(8,128)}, u32[]{:S(2)}) copy-start(s32[256,256]{1,0:T(8,128)} %get-tuple-element.43) | copy-start | bytes 786436
  58.5 5.1 %copy-start.4 = (s32[256,256]{1,0:T(8,128)S(1)}, s32[256,256]{1,0:T(8,128)}, u32[]{:S(2)}) copy-start(s32[256,256]{1,0:T(8,128)} %get-tuple-element.44) | copy-start | bytes 786436
  58.5 21.5 %all-to-all-start = ((f32[16,16,1024]{2,1,0:T(8,128)}), f32[16,16,1024]{2,1,0:T(8,128)S(1)}, u32[]{:S(2)}, u32[]{:S(2)}) async-start(f32[16,16,1024]{2,1,0:T(8,128)} %get-tuple-element.37), calls=%async_computation | async-start | bytes 2097152 | tf_op jit(solution)/shard_map/all_to_all | solution.py:453
  65.6 1.9 %copy-start.5 = (s32[256,256]{1,0:T(8,128)S(1)}, s32[256,256]{1,0:T(8,128)}, u32[]{:S(2)}) copy-start(s32[256,256]{1,0:T(8,128)} %get-tuple-element.45) | copy-start | bytes 786436
  85.7 20.2 %all-to-all-start.3 = ((f32[16,16,1024]{2,1,0:T(8,128)}), f32[16,16,1024]{2,1,0:T(8,128)S(1)}, u32[]{:S(2)}, u32[]{:S(2)}) async-start(f32[16,16,1024]{2,1,0:T(8,128)} %bitcast.15), calls=%async_computation.3 | async-start | bytes 2097152 | tf_op jit(solution)/shard_map/all_to_all | solution.py:453
  105.9 20.2 %all-to-all-start.2 = ((f32[16,16,1024]{2,1,0:T(8,128)}), f32[16,16,1024]{2,1,0:T(8,128)S(1)}, u32[]{:S(2)}, u32[]{:S(2)}) async-start(f32[16,16,1024]{2,1,0:T(8,128)} %bitcast.14), calls=%async_computation.2 | async-start | bytes 2097152 | tf_op jit(solution)/shard_map/all_to_all | solution.py:453

commit v2 on v1

--- a/solution.py
+++ b/solution.py
@@ -50,8 +50,8 @@
     return pltpu.with_memory_space_constraint(x, pltpu.HBM)
 
 
-def pack_kernel(incident, phase, *refs):
-    outs, edge, sems, edge_sems = refs[:-3], refs[-3], refs[-2], refs[-1]
+def pack_kernel(chunk, incident, phase, *refs):
+    outs, edge, sems, edge_sems = refs[:2], refs[2], refs[3], refs[4]
     rows = incident.shape[2] // COLS
     sides = ((rows - BELOW, BELOW), (0, ABOVE))
     edges = [
@@ -63,48 +63,45 @@
     for c in edges:
         c.start()
     copies = []
-    for chunk in range(CHUNKS):
-        for side, (first, count) in enumerate(sides):
-            for i in range(count):
-                at = (first + i) * COLS + chunk * W
-                for part in range(2):
-                    copies.append(
-                        pltpu.make_async_copy(
-                            incident.at[part, :, at : at + W],
-                            outs[2 * chunk + side].at[16 * part : 16 * part + 16, i * W : i * W + W],
-                            sems.at[chunk, side, i, part],
-                        )
+    for side, (first, count) in enumerate(sides):
+        for i in range(count):
+            at = (first + i) * COLS + chunk * W
+            for part in range(2):
+                copies.append(
+                    pltpu.make_async_copy(
+                        incident.at[part, :, at : at + W],
+                        outs[side].at[16 * part : 16 * part + 16, i * W : i * W + W],
+                        sems.at[side, i, part],
                     )
-                    copies[-1].start()
+                )
+                copies[-1].start(priority=(i + part) % 2)
     for c in edges:
         c.wait()
-    for chunk in range(CHUNKS):
-        for side, (first, count) in enumerate(sides):
-            out = outs[2 * chunk + side]
-            for t in range(TILES):
-                at = count * W + t * 128
-                out[:, at : at + 128] = jnp.zeros((32, 128), jnp.float32)
-                for i in range(count):
-                    lane = i * COLS + chunk * W + t * 128
-                    out[3 * i : 3 * i + 3, at : at + 128] = edge[side, :, lane : lane + 128].astype(jnp.float32)
+    for side, (first, count) in enumerate(sides):
+        for t in range(TILES):
+            at = count * W + t * 128
+            outs[side][:, at : at + 128] = jnp.zeros((32, 128), jnp.float32)
+            for i in range(count):
+                lane = i * COLS + chunk * W + t * 128
+                outs[side][3 * i : 3 * i + 3, at : at + 128] = edge[side, :, lane : lane + 128].astype(jnp.float32)
     for c in copies:
         c.wait()
 
 
-def pack(incident, phase):
-    widths = [BELOW * W + TILES * 128, ABOVE * W + TILES * 128] * CHUNKS
+def pack(incident, phase, chunk):
+    widths = [BELOW * W + TILES * 128, ABOVE * W + TILES * 128]
     return pl.pallas_call(
-        pack_kernel,
+        functools.partial(pack_kernel, chunk),
         out_shape=tuple(jax.ShapeDtypeStruct((32, w), jnp.float32) for w in widths),
         in_specs=[pl.BlockSpec(memory_space=pl.ANY)] * 2,
-        out_specs=(pl.BlockSpec(memory_space=pltpu.VMEM),) * len(widths),
+        out_specs=(pl.BlockSpec(memory_space=pltpu.VMEM),) * 2,
         scratch_shapes=[
             pltpu.VMEM((2, 3, ABOVE * COLS), jnp.int32),
-            pltpu.SemaphoreType.DMA((CHUNKS, 2, ABOVE, 2)),
+            pltpu.SemaphoreType.DMA((2, ABOVE, 2)),
             pltpu.SemaphoreType.DMA((2,)),
         ],
         compiler_params=pltpu.CompilerParams(vmem_limit_bytes=8 * 1024 * 1024),
-        cost_estimate=pl.CostEstimate(flops=0, bytes_accessed=2 * 1024 * 1024, transcendentals=0),
+        cost_estimate=pl.CostEstimate(flops=0, bytes_accessed=1024 * 1024, transcendentals=0),
         name="pack",
     )(in_hbm(incident), in_hbm(phase))
 
@@ -414,7 +411,7 @@
         for r in range(4):
             at = (4 * b + r) * COLS + chunk * W
             copies.append(pltpu.make_async_copy(block.at[b, :, r * W : r * W + W], out.at[:, at : at + W], sems.at[b, r]))
-            copies[-1].start()
+            copies[-1].start(priority=(b + r) % 2)
     for c in copies:
         c.wait()
 
@@ -455,10 +452,9 @@
 
 def on_device(incident, detuning, phase_table, response, counts):
     span = incident.shape[2]
-    edges = pack(incident, phase_table)
     below, above = [], []
     for chunk in range(CHUNKS):
-        lower, upper = edges[2 * chunk], edges[2 * chunk + 1]
+        lower, upper = pack(incident, phase_table, chunk)
         below.append(passed_along(lower, "lat", 1))
         above.append(passed_along(upper, "lat", -1))
     angle = -0.5 * detuning[None, :] * jnp.array([-10.0, -9.0, -8.0, -7.0, -6.0, -5.0, -4.0, -3.0, 8.0], jnp.float32)[:, None]

time: 128 us -> 128 us (level)
  matrix products: 21 us -> 19.5 us
    ppermute x4, waiting for transfers between devices: 17 us -> 15.2 us  [passed_along(): lax.ppermute(x, axis, [(i, (i + by) % devices) for i in range(devices)])]
    pallas_call x1 -> x2, Pallas kernels: 2.18 us -> 3.02 us  [pack(): pl.pallas_call(functools.partial(pack_kernel, chunk), out_shape=tuple((ja...]
  transfers between devices with their start and end apart: 8 -> 8, of which waited for: 6 -> 6; matrix products, arithmetic and copies ran while one was open for 14% -> 13% of each run, Pallas kernels for 17% -> 19%
where the time goes in v2:
time: 128 us; the launch traced here: 127 us
  waiting for transfers between devices  43 us (34%)
  starting transfers between devices  30.2 us (24%)
  Pallas kernels  29.5 us (23%)
  matrix products  19.5 us (15%)
  local copies, waits for them, and re-layouts  3.29 us (3%)
    all_to_all x4, waiting for transfers between devices, exchange(): return lax.all_to_all(x, 'ang', split_axis=0, concat_axis=0, tiled=True)  27.7 us
    all_to_all x4, starting transfers between devices, exchange(): return lax.all_to_all(x, 'ang', split_axis=0, concat_axis=0, tiled=True)  18.8 us
    pallas_call x3, Pallas kernels, sweep(): pl.pallas_call(functools.partial(sweep_kernel, mode, chunk), out_shape=tu...  17.7 us
    ppermute x4, waiting for transfers between devices, passed_along(): lax.ppermute(x, axis, [(i, (i + by) % devices) for i in range(devices)])  15.2 us
    ppermute x4, starting transfers between devices, passed_along(): lax.ppermute(x, axis, [(i, (i + by) % devices) for i in range(devices)])  11.4 us
    dot_general x12, matrix products, deconvolve(): lax.dot_general(scaled, measured / blurred, (((0,), (0,)), ((), ())), pre...  10 us
    dot_general x12, matrix products, deconvolve(): jnp.dot(response, estimate, precision=lax.Precision.HIGH, preferred_eleme...  9.52 us
    pallas_call x1, Pallas kernels, merge(): pl.pallas_call(merge_kernel, grid=(1,), out_shape=jax.ShapeDtypeStruct((2...  5.73 us
  transfers between devices with their start and end apart: 8, of which 6 were waited for; matrix products, arithmetic and copies ran while one was open for 13% of the time, Pallas kernels for 19%

profile of v2, /device:TPU:24, one launch (start us, length us, event | category | flops | bytes accessed | tf_op | source)
XLA Modules:
  0.0 127.0 jit_solution(5744800513752797744)
XLA Ops:
  0.6 0.0 copy-start.10
  0.6 0.0 copy-start
  0.7 0.0 copy-start.11
  0.7 1.5 %pack.2 = (f32[32,2048]{1,0:T(8,128)S(1)}, f32[32,2560]{1,0:T(8,128)S(1)}) custom-call(f32[2,16,32768]{2,1,0:T(8,128)} %refs_0_.3, s32[3,32768]{1,0:T(4,128)} %phase.9), custom_call_target="tpu_custom_call" | custom-call | bytes 1048576 | tf_op jit(solution)/shard_map/pack/pallas_call | solution.py:93
  2.2 0.8 collective-permute-start.1
  3.0 4.9 %collective-permute-start = (f32[32,2048]{1,0:T(8,128)S(1)}, f32[32,2048]{1,0:T(8,128)S(1)}, u32[]{:S(2)}, u32[]{:S(2)}) collective-permute-start(f32[32,2048]{1,0:T(8,128)S(1)} %get-tuple-element.21), channel_id=1, source_target_pairs={{0,16},{16,32},{32,48},{48,64},{64,80},{80,96},{96,112},{112,0},{1... | collective-permute-start | bytes 786440 | tf_op jit(solution)/shard_map/ppermute | solution.py:28
  7.9 0.0 copy-done.11
  7.9 0.0 copy-done.10
  7.9 0.2 multiply_cosine_fusion
  8.1 0.1 broadcast_in_dim.2.refs_1_.gauge_in
  8.2 0.0 copy-done
  8.2 0.0 copy-start.2
  8.3 6.1 %sweep.3 = (f32[2,48,2,16,128]{4,3,2,1,0:T(8,128)S(1)}, f32[16,16,1024]{2,1,0:T(8,128)S(1)}, f32[2,2,88,128]{3,2,1,0:T(8,128)}, f32[5,2,2,88,128]{4,3,2,1,0:T(8,...) custom-call(s32[3,32768]{1,0:T(4,128)S(1)} %copy-done, ...), custom_call_target="tpu_custom_call" | custom-call | flops 23592960 | bytes 8388608 | tf_op jit(solution)/shard_map/sweep/pallas_call | solution.py:353
  14.4 0.0 collective-permute-done.refs_0_
  14.4 1.0 collective-permute-done.1.refs_1_
  15.3 2.7 %sweep.4 = (f32[2,48,2,16,128]{4,3,2,1,0:T(8,128)}, f32[2,18,2,16,128]{4,3,2,1,0:T(8,128)}, f32[16,16,1024]{2,1,0:T(8,128)}, f32[2,2,88,128]{3,2,1,0:T(8,128)}, ...) custom-call(s32[3,32768]{1,0:T(4,128)S(1)} %copy-done, ...), custom_call_target="tpu_custom_call", output_to_operand_aliasing={{4}: (6, {}), {5}: (7, {}), {6}: (8, {})} | custom-call | flops 8847360 | bytes 8388608 | tf_op jit(solution)/shard_map/sweep/pallas_call | solution.py:353
  18.1 6.4 %all-to-all-start.1 = ((f32[16,16,1024]{2,1,0:T(8,128)}), f32[16,16,1024]{2,1,0:T(8,128)S(1)}, u32[]{:S(2)}, u32[]{:S(2)}) async-start(f32[16,16,1024]{2,1,0:T(8,128)} %get-tuple-element.38), calls=%async_computation.1 | async-start | bytes 2097152 | tf_op jit(solution)/shard_map/all_to_all | solution.py:450
  24.4 0.0 copy-start.3
  24.4 1.5 %pack.3 = (f32[32,2048]{1,0:T(8,128)S(1)}, f32[32,2560]{1,0:T(8,128)S(1)}) custom-call(f32[2,16,32768]{2,1,0:T(8,128)} %refs_0_.3, s32[3,32768]{1,0:T(4,128)} %phase.9), custom_call_target="tpu_custom_call" | custom-call | bytes 1048576 | tf_op jit(solution)/shard_map/pack/pallas_call | solution.py:93
  25.9 0.1 collective-permute-start.3
  26.0 5.6 %collective-permute-start.2 = (f32[32,2048]{1,0:T(8,128)S(1)}, f32[32,2048]{1,0:T(8,128)S(1)}, u32[]{:S(2)}, u32[]{:S(2)}) collective-permute-start(f32[32,2048]{1,0:T(8,128)S(1)} %get-tuple-element.31), channel_id=1, source_target_pairs={{0,16},{16,32},{32,48},{48,64},{64,80},{80,96},{96,112},{112,0},{1... | collective-permute-start | bytes 786440 | tf_op jit(solution)/shard_map/ppermute | solution.py:28
  31.7 0.0 copy-done.3
  31.7 0.0 copy-start.1
  31.7 2.8 %fusion.24 = (s32[256,256]{1,0:T(8,128)S(1)}, s32[256,256]{1,0:T(8,128)S(1)}, s32[256,256]{1,0:T(8,128)}, s32[256,256]{1,0:T(8,128)}, s32[256,256]{1,0:T(8,128)}...) fusion(s32[256,2048]{1,0:T(8,128)} %param.10), kind=kLoop, calls=%fused_computation.55 | loop fusion | bytes 4194304 | tf_op jit(solution)/shard_map/slice | solution.py:467
  34.5 7.9 %collective-permute-done.2.refs_2_ = f32[32,2048]{1,0:T(8,128)S(1)} collective-permute-done((f32[32,2048]{1,0:T(8,128)S(1)}, f32[32,2048]{1,0:T(8,128)S(1)}, u32[]{:S(2)}, u32[]{:S(2)}) %collective-permute-start.2) | collective-permute-done | bytes 262176 | tf_op jit(solution)/shard_map/ppermute | solution.py:28
  42.4 6.4 %collective-permute-done.3.refs_3_ = f32[32,2560]{1,0:T(8,128)S(1)} collective-permute-done((f32[32,2560]{1,0:T(8,128)S(1)}, f32[32,2560]{1,0:T(8,128)S(1)}, u32[]{:S(2)}, u32[]{:S(2)}) %collective-permute-start.3) | collective-permute-done | bytes 327712 | tf_op jit(solution)/shard_map/ppermute | solution.py:28
  48.8 0.0 copy-done.2
  48.8 8.9 %sweep.5 = (f32[2,64,2,16,128]{4,3,2,1,0:T(8,128)}, f32[16,16,1024]{2,1,0:T(8,128)}, f32[2,2,88,128]{3,2,1,0:T(8,128)}) custom-call(s32[3,32768]{1,0:T(4,128)S(1)} %copy-done.1, f32[2,16,32768]{2,1,0:T(8,128)} %refs_0_.3, f32[9,2,16,128]{3,2,1,0:T(8,128)S(1)} %broadcast_in_dim.2.refs_1_.gauge_in, f32[32,2048]{1,0:T(8,128)S(1)} %collective-permute-done.2.refs_2_, ...), custom_call_target="tpu_custom_call" | custom-call | flops 31457280 | bytes 8388608 | tf_op jit(solution)/shard_map/sweep/pallas_call | solution.py:353
  57.7 0.0 all-to-all-done.1
  57.7 5.1 %all-to-all-start = ((f32[16,16,1024]{2,1,0:T(8,128)}), f32[16,16,1024]{2,1,0:T(8,128)S(1)}, u32[]{:S(2)}, u32[]{:S(2)}) async-start(f32[16,16,1024]{2,1,0:T(8,128)} %get-tuple-element.37), calls=%async_computation | async-start | bytes 2097152 | tf_op jit(solution)/shard_map/all_to_all | solution.py:450
  62.8 1.7 %fusion.23 = f32[256,1024]{1,0:T(8,128)S(1)} fusion(f32[256,1024]{1,0:T(8,128)S(1)} %bitcast.88, f32[256,256]{1,0:T(8,128)S(1)} %copy-done.3, s32[256,256]{1,0:T(8,128)S(1)} %copy-done.6, s32[256,256]{1,0:T(8,128)S(1)} %copy-done.7, s32[256,256]{1,0:T(8,128)} %get-tuple-element.44, s32[256,256]{1,0:T(8,128)} %get-tuple-element.45), kind=kOutput, calls=%fused_computation.47 | convolution fusion | flops 404226048 | bytes 3407872 | tf_op jit(solution)/shard_map/dot_general | solution.py:437
  64.6 0.7 convolution_multiply_fusion.11
  65.3 0.3 copy-done.8
  65.5 0.1 copy-done.9
  65.6 0.7 fusion.21
  66.3 0.7 convolution_multiply_fusion.10
  67.0 0.7 fusion.19
  67.7 0.7 convolution_multiply_fusion.9
  68.4 0.7 fusion.17
  69.1 0.7 convolution_multiply_fusion.8
  69.7 0.7 fusion.15
  70.4 0.7 convolution_multiply_fusion.7
  71.1 0.7 fusion.13
  71.8 1.6 %convolution_multiply_fusion.6 = f32[256,1024]{1,0:T(8,128)} fusion(f32[256,1024]{1,0:T(8,128)S(1)} %convolution_multiply_fusion.7, f32[256,1024]{1,0:T(8,128)S(1)} %fusion.13, f32[256,256]{1,0:T(8,128)S(1)} %copy-done.3, f32[256]{0:T(256)S(1)} %reduce_sum.9), kind=kOutput, calls=%fused_computation.24 | convolution fusion | flops 402980864 | bytes 3408896 | tf_op jit(solution)/shard_map/dot_general | solution.py:438
  73.5 5.7 %all-to-all-done = f32[16,16,1024]{2,1,0:T(8,128)S(1)} async-done(((f32[16,16,1024]{2,1,0:T(8,128)}), f32[16,16,1024]{2,1,0:T(8,128)S(1)}, u32[]{:S(2)}, u32[]{:S(2)}) %all-to-all-start) | async-done | bytes 1048608 | tf_op jit(solution)/shard_map/all_to_all | solution.py:450
  79.2 0.7 fusion.11
  79.9 0.7 convolution_multiply_fusion.5
  80.6 0.7 fusion.9
  81.3 0.7 convolution_multiply_fusion.4
  81.9 0.7 fusion.7
  82.6 0.9 convolution_multiply_fusion.3
  83.5 0.7 fusion.5
  84.2 0.7 convolution_multiply_fusion.2
  84.9 3.7 %all-to-all-start.3 = ((f32[16,16,1024]{2,1,0:T(8,128)}), f32[16,16,1024]{2,1,0:T(8,128)S(1)}, u32[]{:S(2)}, u32[]{:S(2)}) async-start(f32[16,16,1024]{2,1,0:T(8,128)} %bitcast.15), calls=%async_computation.3 | async-start | bytes 2097152 | tf_op jit(solution)/shard_map/all_to_all | solution.py:450
  88.6 0.7 fusion.3
  89.3 0.7 convolution_multiply_fusion.1
  90.0 0.7 fusion.1
  90.7 1.6 %convolution_multiply_fusion = f32[256,1024]{1,0:T(8,128)} fusion(f32[256,1024]{1,0:T(8,128)S(1)} %convolution_multiply_fusion.1, f32[256,1024]{1,0:T(8,128)S(1)} %fusion.1, f32[256,256]{1,0:T(8,128)S(1)} %copy-done.3, f32[256]{0:T(256)S(1)} %reduce_sum.9), kind=kOutput, calls=%fused_computation | convolution fusion | flops 402980864 | bytes 3408896 | tf_op jit(solution)/shard_map/dot_general | solution.py:438
  92.3 12.8 %all-to-all-done.3.block = f32[16,16,1024]{2,1,0:T(8,128)S(1)} async-done(((f32[16,16,1024]{2,1,0:T(8,128)}), f32[16,16,1024]{2,1,0:T(8,128)S(1)}, u32[]{:S(2)}, u32[]{:S(2)}) %all-to-all-start.3) | async-done | bytes 1048608 | tf_op jit(solution)/shard_map/all_to_all | solution.py:450
  105.1 3.7 %all-to-all-start.2 = ((f32[16,16,1024]{2,1,0:T(8,128)}), f32[16,16,1024]{2,1,0:T(8,128)S(1)}, u32[]{:S(2)}, u32[]{:S(2)}) async-start(f32[16,16,1024]{2,1,0:T(8,128)} %bitcast.14), calls=%async_computation.2 | async-start | bytes 2097152 | tf_op jit(solution)/shard_map/all_to_all | solution.py:450
  108.7 5.7 %merge.1 = f32[2,16,32768]{2,1,0:T(8,128)} custom-call(f32[9,2,16,128]{3,2,1,0:T(8,128)} %copy-done.2, f32[2,48,2,16,128]{4,3,2,1,0:T(8,128)} %get-tuple-element.29.inner, f32[2,18,2,16,128]{4,3,2,1,0:T(8,128)} %get-tuple-element.30.border, f32[2,64,2,16,128]{4,3,2,1,0:T(8,128)} %get-tuple-element.33.whole, f32[2,2,88,128]{3,2,1,0:T(8,128)} %get-tuple-element.34.last_inner, ...), custom_call_target="tpu_custom_call" | custom-call | bytes 8388608 | tf_op jit(solution)/shard_map/merge/pallas_call | solution.py:395
  114.5 1.5 %place.2.refs_0_ = f32[16,32768]{1,0:T(8,128)} custom-call(f32[16,16,1024]{2,1,0:T(8,128)S(1)} %all-to-all-done.3.block), custom_call_target="tpu_custom_call" | custom-call | bytes 4194304 | tf_op jit(solution)/shard_map/place/pallas_call | solution.py:422
  116.0 9.2 %all-to-all-done.2.block = f32[16,16,1024]{2,1,0:T(8,128)S(1)} async-done(((f32[16,16,1024]{2,1,0:T(8,128)}), f32[16,16,1024]{2,1,0:T(8,128)S(1)}, u32[]{:S(2)}, u32[]{:S(2)}) %all-to-all-start.2) | async-done | bytes 1048608 | tf_op jit(solution)/shard_map/all_to_all | solution.py:450
  125.3 1.5 %place.3 = f32[16,32768]{1,0:T(8,128)} custom-call(f32[16,16,1024]{2,1,0:T(8,128)S(1)} %all-to-all-done.2.block, f32[16,32768]{1,0:T(8,128)} %place.2.refs_0_), custom_call_target="tpu_custom_call", output_to_operand_aliasing={{}: (1, {})} | custom-call | bytes 4194304 | tf_op jit(solution)/shard_map/place/pallas_call | solution.py:422
  (14 shorter events, 0.1 us)
Async XLA Ops:
  0.6 7.3 %copy-start.10 = (f32[9]{0:T(128)S(1)}, f32[9]{0:T(128)}, u32[]{:S(2)}) copy-start(f32[9]{0:T(128)} %constant.8.clone) | copy-start | bytes 112
  0.6 7.6 %copy-start = (s32[3,32768]{1,0:T(4,128)S(1)}, s32[3,32768]{1,0:T(4,128)}, u32[]{:S(2)}) copy-start(s32[3,32768]{1,0:T(4,128)} %phase.9) | copy-start | bytes 1179652
  0.7 7.2 %copy-start.11 = (f32[16]{0:T(128)S(1)}, f32[16]{0:T(128)}, u32[]{:S(2)}) copy-start(f32[16]{0:T(128)} %param.7) | copy-start | bytes 196
  2.2 13.1 %collective-permute-start.1 = (f32[32,2560]{1,0:T(8,128)S(1)}, f32[32,2560]{1,0:T(8,128)S(1)}, u32[]{:S(2)}, u32[]{:S(2)}) collective-permute-start(f32[32,2560]{1,0:T(8,128)S(1)} %get-tuple-element.22), channel_id=1, source_target_pairs={{0,112},{16,0},{32,16},{48,32},{64,48},{80,64},{96,80},{112,96},{1... | collective-permute-start | bytes 983048 | tf_op jit(solution)/shard_map/ppermute | solution.py:28
  3.0 11.4 %collective-permute-start = (f32[32,2048]{1,0:T(8,128)S(1)}, f32[32,2048]{1,0:T(8,128)S(1)}, u32[]{:S(2)}, u32[]{:S(2)}) collective-permute-start(f32[32,2048]{1,0:T(8,128)S(1)} %get-tuple-element.21), channel_id=1, source_target_pairs={{0,16},{16,32},{32,48},{48,64},{64,80},{80,96},{96,112},{112,0},{1... | collective-permute-start | bytes 786440 | tf_op jit(solution)/shard_map/ppermute | solution.py:28
  8.2 40.6 %copy-start.2 = (f32[9,2,16,128]{3,2,1,0:T(8,128)}, f32[9,2,16,128]{3,2,1,0:T(8,128)S(1)}, u32[]{:S(2)}) copy-start(f32[9,2,16,128]{3,2,1,0:T(8,128)S(1)} %broadcast_in_dim.2.refs_1_.gauge_in) | copy-start | bytes 442372
  18.1 39.6 %all-to-all-start.1 = ((f32[16,16,1024]{2,1,0:T(8,128)}), f32[16,16,1024]{2,1,0:T(8,128)S(1)}, u32[]{:S(2)}, u32[]{:S(2)}) async-start(f32[16,16,1024]{2,1,0:T(8,128)} %get-tuple-element.38), calls=%async_computation.1 | async-start | bytes 2097152 | tf_op jit(solution)/shard_map/all_to_all | solution.py:450
  24.4 7.2 %copy-start.3 = (f32[256,256]{1,0:T(8,128)S(1)}, f32[256,256]{1,0:T(8,128)}, u32[]{:S(2)}) copy-start(f32[256,256]{1,0:T(8,128)} %param.9) | copy-start | bytes 786436
  25.9 22.9 %collective-permute-start.3 = (f32[32,2560]{1,0:T(8,128)S(1)}, f32[32,2560]{1,0:T(8,128)S(1)}, u32[]{:S(2)}, u32[]{:S(2)}) collective-permute-start(f32[32,2560]{1,0:T(8,128)S(1)} %get-tuple-element.32), channel_id=1, source_target_pairs={{0,112},{16,0},{32,16},{48,32},{64,48},{80,64},{96,80},{112,96},{1... | collective-permute-start | bytes 983048 | tf_op jit(solution)/shard_map/ppermute | solution.py:28
  26.0 16.3 %collective-permute-start.2 = (f32[32,2048]{1,0:T(8,128)S(1)}, f32[32,2048]{1,0:T(8,128)S(1)}, u32[]{:S(2)}, u32[]{:S(2)}) collective-permute-start(f32[32,2048]{1,0:T(8,128)S(1)} %get-tuple-element.31), channel_id=1, source_target_pairs={{0,16},{16,32},{32,48},{48,64},{64,80},{80,96},{96,112},{112,0},{1... | collective-permute-start | bytes 786440 | tf_op jit(solution)/shard_map/ppermute | solution.py:28
  31.7 17.1 %copy-start.1 = (s32[3,32768]{1,0:T(4,128)S(1)}, s32[3,32768]{1,0:T(4,128)}, u32[]{:S(2)}) copy-start(s32[3,32768]{1,0:T(4,128)} %phase.9) | copy-start | bytes 1179652
  57.7 5.1 %copy-start.6 = (s32[256,256]{1,0:T(8,128)S(1)}, s32[256,256]{1,0:T(8,128)}, u32[]{:S(2)}) copy-start(s32[256,256]{1,0:T(8,128)} %get-tuple-element.42) | copy-start | bytes 786436
  57.7 5.1 %copy-start.7 = (s32[256,256]{1,0:T(8,128)S(1)}, s32[256,256]{1,0:T(8,128)}, u32[]{:S(2)}) copy-start(s32[256,256]{1,0:T(8,128)} %get-tuple-element.43) | copy-start | bytes 786436
  57.7 21.5 %all-to-all-start = ((f32[16,16,1024]{2,1,0:T(8,128)}), f32[16,16,1024]{2,1,0:T(8,128)S(1)}, u32[]{:S(2)}, u32[]{:S(2)}) async-start(f32[16,16,1024]{2,1,0:T(8,128)} %get-tuple-element.37), calls=%async_computation | async-start | bytes 2097152 | tf_op jit(solution)/shard_map/all_to_all | solution.py:450
  64.6 1.0 copy-start.8
  64.6 1.0 copy-start.9
  71.8 7.4 %copy-start.4 = (s32[256,256]{1,0:T(8,128)S(1)}, s32[256,256]{1,0:T(8,128)}, u32[]{:S(2)}) copy-start(s32[256,256]{1,0:T(8,128)} %get-tuple-element.46) | copy-start | bytes 786436
  71.8 7.3 %copy-start.5 = (s32[256,256]{1,0:T(8,128)S(1)}, s32[256,256]{1,0:T(8,128)}, u32[]{:S(2)}) copy-start(s32[256,256]{1,0:T(8,128)} %get-tuple-element.47) | copy-start | bytes 786436
  84.9 20.2 %all-to-all-start.3 = ((f32[16,16,1024]{2,1,0:T(8,128)}), f32[16,16,1024]{2,1,0:T(8,128)S(1)}, u32[]{:S(2)}, u32[]{:S(2)}) async-start(f32[16,16,1024]{2,1,0:T(8,128)} %bitcast.15), calls=%async_computation.3 | async-start | bytes 2097152 | tf_op jit(solution)/shard_map/all_to_all | solution.py:450
  105.1 20.2 %all-to-all-start.2 = ((f32[16,16,1024]{2,1,0:T(8,128)}), f32[16,16,1024]{2,1,0:T(8,128)S(1)}, u32[]{:S(2)}, u32[]{:S(2)}) async-start(f32[16,16,1024]{2,1,0:T(8,128)} %bitcast.14), calls=%async_computation.2 | async-start | bytes 2097152 | tf_op jit(solution)/shard_map/all_to_all | solution.py:450
